TPU v7x, 256 devices: a whole 4x4x8 slice. The times are simulated.
256 devices in a mesh: band: 64 (over x, z, core), segment: 4 (over y).
Axes of the slice: x: 4, y: 4, z: 8, core: 2. Of those that a mesh axis runs over, the one named last changes fastest.
Arguments:
- fields: bfloat16 [8, 1024, 64, 256], P(None, 'band'), may hold values from -6 to 6
- land_sea: int32 [1024, 64], P('band'), may hold values from 0 to 1, as said below
- conv_kernel: bfloat16 [4, 7, 7, 256], P('segment'), may hold values from -0.875 to 0.875
- conv_bias: bfloat16 [4, 256], P('segment'), may hold values from -3 to 3
- norm_gain: bfloat16 [4, 256], P('segment'), may hold values from 0.5 to 1.5
- norm_shift: bfloat16 [4, 256], P('segment'), may hold values from -3 to 3
- up_proj: bfloat16 [4, 256, 1024], P('segment'), may hold values from -0.375 to 0.375
- up_bias: bfloat16 [4, 1024], P('segment'), may hold values from -3 to 3
- down_proj: bfloat16 [4, 1024, 256], P('segment'), may hold values from -0.1875 to 0.1875
- down_bias: bfloat16 [4, 256], P('segment'), may hold values from -3 to 3
Outputs:
- segment_out: bfloat16 [4, 8, 1024, 64, 256], P('segment', None, 'band')
Inputs may be any that keep to these rules, and one draw needn't show every extreme that they name: `land_sea`: each index of band's 16 x 64 cells hold at most 768 wet cells, and some index holds exactly 768.
All inputs are finite; a program needn't handle non-finite values.
Results may differ from a plain program's by a relative error of at most 0.01.
Values may be sent and summed in bfloat16 or wider, within the bound.
A program may use at most 64 MiB of HBM per device.

v0:
```python
import jax
import jax.numpy as jnp
from jax import lax
from jax.sharding import PartitionSpec as P


def extended(block, sides, width):
    for axis, dim in sides:
        count = lax.axis_size(axis)
        forward = [(i, i + 1) for i in range(count - 1)]
        backward = [(target, source) for source, target in forward]
        low = lax.ppermute(
            lax.slice_in_dim(block, block.shape[dim] - width, None, axis=dim), axis, forward
        )
        high = lax.ppermute(lax.slice_in_dim(block, 0, width, axis=dim), axis, backward)
        block = jnp.concatenate([low, block, high], axis=dim)
    return block


def passed_along(array, axis, by):
    length = lax.axis_size(axis)
    pairs = [(i, i + by) for i in range(length) if 0 <= i + by < length]
    return lax.ppermute(array, axis, pairs)


def layer_norm(summed, gain, offset):
    centre = jnp.mean(summed, axis=-1, keepdims=True)
    deviation = summed - centre
    variance = jnp.mean(deviation * deviation, axis=-1, keepdims=True)
    return deviation * lax.rsqrt(variance + 1e-06) * gain.astype(jnp.float32) + offset.astype(
        jnp.float32
    )


def pointwise(normed, up_w, up_b, down_w, down_b):
    hidden = jax.nn.gelu(
        jnp.dot(normed, up_w, preferred_element_type=jnp.float32) + up_b.astype(jnp.float32),
        approximate=False,
    ).astype(jnp.bfloat16)
    return jnp.dot(hidden, down_w, preferred_element_type=jnp.float32) + down_b.astype(jnp.float32)


def section(state, mask_f, params):
    kernel, conv_b, norm_g, norm_o, up_w, up_b, down_w, down_b = params
    row_count, col_count, channels = state.shape
    reach = kernel.shape[0] // 2
    padded_rows = extended(state, (("band", 0),), reach)
    wrapped = jnp.concatenate(
        [padded_rows[:, col_count - reach :], padded_rows, padded_rows[:, :reach]], axis=1
    )
    summed = jnp.zeros(state.shape, jnp.float32) + conv_b.astype(jnp.float32)
    for row_off in range(2 * reach + 1):
        for col_off in range(2 * reach + 1):
            window = wrapped[row_off : row_off + row_count, col_off : col_off + col_count]
            summed = summed + window.astype(jnp.float32) * kernel[row_off, col_off].astype(
                jnp.float32
            )
    normed = (
        layer_norm(summed, norm_g, norm_o)
        .astype(jnp.bfloat16)
        .reshape(row_count * col_count, channels)
    )
    update = pointwise(normed, up_w, up_b, down_w, down_b)
    merged = (state.astype(jnp.float32) + update.reshape(state.shape)) * mask_f[:, :, None]
    return merged.astype(jnp.bfloat16)


def on_device(
    fields,
    land_sea,
    conv_kernel,
    conv_bias,
    norm_gain,
    norm_shift,
    up_proj,
    up_bias,
    down_proj,
    down_bias,
):
    mask_f = land_sea.astype(jnp.float32)
    segment_no = lax.axis_index("segment")
    segment_count = lax.axis_size("segment")
    batch_size = fields.shape[0]
    params = tuple(
        (
            piece[0]
            for piece in (
                conv_kernel,
                conv_bias,
                norm_gain,
                norm_shift,
                up_proj,
                up_bias,
                down_proj,
                down_bias,
            )
        )
    )
    outputs = jnp.zeros(fields.shape, jnp.bfloat16)
    incoming = jnp.zeros(fields.shape[1:], jnp.bfloat16)

    def tick(tick_no, carry):
        incoming, outputs = carry
        fresh = lax.dynamic_index_in_dim(
            fields, jnp.minimum(tick_no, batch_size - 1), 0, keepdims=False
        )
        fresh = (fresh.astype(jnp.float32) * mask_f[:, :, None]).astype(jnp.bfloat16)
        current = jnp.where(segment_no == 0, fresh, incoming)
        result = section(current, mask_f, params)
        slot_no = tick_no - segment_no
        is_valid = (slot_no >= 0) & (slot_no < batch_size)
        place = jnp.clip(slot_no, 0, batch_size - 1)
        previous = lax.dynamic_index_in_dim(outputs, place, 0, keepdims=False)
        outputs = lax.dynamic_update_index_in_dim(
            outputs, jnp.where(is_valid, result, previous), place, 0
        )
        incoming = passed_along(result, "segment", 1)
        return (incoming, outputs)

    incoming, outputs = lax.fori_loop(0, batch_size + segment_count - 1, tick, (incoming, outputs))
    return outputs[None]


def solution(mesh):
    in_specs = (
        P(None, "band", None, None),
        P("band", None),
        P("segment", None, None, None),
        P("segment", None),
        P("segment", None),
        P("segment", None),
        P("segment", None, None),
        P("segment", None),
        P("segment", None, None),
        P("segment", None),
    )
    out_specs = P("segment", None, "band", None, None)
    return jax.shard_map(
        on_device, mesh=mesh, in_specs=in_specs, out_specs=out_specs, check_vma=False
    )
```

profile of v0, /device:TPU:29, one launch (start us, length us, event | category | flops | bytes accessed | tf_op | source)
XLA Modules:
  0.0 526.2 jit_solution(14673501981908341790)
XLA Ops:
  6.8 519.4 %while.16 = (s32[]{:T(128)}, bf16[16,64,256]{2,1,0:T(8,128)(2,1)S(1)}, bf16[8,16,64,256]{3,2,1,0:T(8,128)(2,1)}, pred[]{:T(512)}, bf16[8,16,64,256]{3,2,1,0:T(8,...) while((s32[]{:T(128)}, ...), condition=%wide.region_3.4_spmd, body=%wide.region_0.3_spmd.sunk | while | flops 1197108480 | bytes 40498072 | solution.py:120
  19.3 9.3 %fusion.95 = (f32[16,64]{1,0:T(8,128)S(1)}, f32[16,64,256]{2,1,0:T(8,128)S(1)}) fusion(f32[256]{0:T(256)S(1)} %bitcast.215, bf16[22,67,256]{2,1,0:T(8,128)(2,1)S(1)} %get-tuple-element.534, f32[256]{0:T(256)S(1)} %bitcast.216, f32[256]{0:T(256)S(1)} %bitcast.217, f32[256]{0:T(256)S(1)} %bitcast.218, ...), kind=kLoop, calls=%fused_computation.158.clone.1 | loop fusion | flops 40369152 | bytes 23844864 | tf_op jit(solution)/shard_map/while/body/eval_jaxpr/reduce_sum | solution.py:27
  29.3 11.0 %convolution_add_fusion.2 = f32[1024,256]{1,0:T(8,128)S(1)} fusion(bf16[1024,256]{1,0:T(8,128)(2,1)} %get-tuple-element.638, bf16[1024,256]{1,0:T(8,128)(2,1)S(1)} %bitcast.182, bf16[256,1024]{1,0:T(8,128)(2,1)} %get-tuple-element.636, f32[1024]{0:T(1024)S(1)} %convert_element_type.1021, f32[256]{0:T(256)S(1)} %convert_element_type.1022), kind=kOutput, calls=%fused_computation.19.clone.1 | convolution fusion | flops 1143209984 | bytes 2626560 | tf_op jit(solution)/shard_map/while/body/eval_jaxpr/dot_general | solution.py:40
  42.8 8.6 %collective-permute-done.2 = bf16[16,64,256]{2,1,0:T(8,128)(2,1)S(1)} collective-permute-done((bf16[16,64,256]{2,1,0:T(8,128)(2,1)S(1)}, bf16[16,64,256]{2,1,0:T(8,128)(2,1)S(1)}, u32[]{:S(2)}, u32[]{:S(2)}) %collective-permute-start.2) | collective-permute-done | bytes 524320 | tf_op jit(solution)/shard_map/while/body/eval_jaxpr/ppermute | solution.py:23
  68.4 9.3 %fusion.95 = (f32[16,64]{1,0:T(8,128)S(1)}, f32[16,64,256]{2,1,0:T(8,128)S(1)}) fusion(f32[256]{0:T(256)S(1)} %bitcast.215, bf16[22,67,256]{2,1,0:T(8,128)(2,1)S(1)} %get-tuple-element.534, f32[256]{0:T(256)S(1)} %bitcast.216, f32[256]{0:T(256)S(1)} %bitcast.217, f32[256]{0:T(256)S(1)} %bitcast.218, ...), kind=kLoop, calls=%fused_computation.158.clone.1 | loop fusion | flops 40369152 | bytes 23844864 | tf_op jit(solution)/shard_map/while/body/eval_jaxpr/reduce_sum | solution.py:27
  78.4 11.0 %convolution_add_fusion.2 = f32[1024,256]{1,0:T(8,128)S(1)} fusion(bf16[1024,256]{1,0:T(8,128)(2,1)} %get-tuple-element.638, bf16[1024,256]{1,0:T(8,128)(2,1)S(1)} %bitcast.182, bf16[256,1024]{1,0:T(8,128)(2,1)} %get-tuple-element.636, f32[1024]{0:T(1024)S(1)} %convert_element_type.1021, f32[256]{0:T(256)S(1)} %convert_element_type.1022), kind=kOutput, calls=%fused_computation.19.clone.1 | convolution fusion | flops 1143209984 | bytes 2626560 | tf_op jit(solution)/shard_map/while/body/eval_jaxpr/dot_general | solution.py:40
  91.9 8.6 %collective-permute-done.2 = bf16[16,64,256]{2,1,0:T(8,128)(2,1)S(1)} collective-permute-done((bf16[16,64,256]{2,1,0:T(8,128)(2,1)S(1)}, bf16[16,64,256]{2,1,0:T(8,128)(2,1)S(1)}, u32[]{:S(2)}, u32[]{:S(2)}) %collective-permute-start.2) | collective-permute-done | bytes 524320 | tf_op jit(solution)/shard_map/while/body/eval_jaxpr/ppermute | solution.py:23
  116.8 9.3 %fusion.95 = (f32[16,64]{1,0:T(8,128)S(1)}, f32[16,64,256]{2,1,0:T(8,128)S(1)}) fusion(f32[256]{0:T(256)S(1)} %bitcast.215, bf16[22,67,256]{2,1,0:T(8,128)(2,1)S(1)} %get-tuple-element.534, f32[256]{0:T(256)S(1)} %bitcast.216, f32[256]{0:T(256)S(1)} %bitcast.217, f32[256]{0:T(256)S(1)} %bitcast.218, ...), kind=kLoop, calls=%fused_computation.158.clone.1 | loop fusion | flops 40369152 | bytes 23844864 | tf_op jit(solution)/shard_map/while/body/eval_jaxpr/reduce_sum | solution.py:27
  126.9 11.0 %convolution_add_fusion.2 = f32[1024,256]{1,0:T(8,128)S(1)} fusion(bf16[1024,256]{1,0:T(8,128)(2,1)} %get-tuple-element.638, bf16[1024,256]{1,0:T(8,128)(2,1)S(1)} %bitcast.182, bf16[256,1024]{1,0:T(8,128)(2,1)} %get-tuple-element.636, f32[1024]{0:T(1024)S(1)} %convert_element_type.1021, f32[256]{0:T(256)S(1)} %convert_element_type.1022), kind=kOutput, calls=%fused_computation.19.clone.1 | convolution fusion | flops 1143209984 | bytes 2626560 | tf_op jit(solution)/shard_map/while/body/eval_jaxpr/dot_general | solution.py:40
  140.3 8.6 %collective-permute-done.2 = bf16[16,64,256]{2,1,0:T(8,128)(2,1)S(1)} collective-permute-done((bf16[16,64,256]{2,1,0:T(8,128)(2,1)S(1)}, bf16[16,64,256]{2,1,0:T(8,128)(2,1)S(1)}, u32[]{:S(2)}, u32[]{:S(2)}) %collective-permute-start.2) | collective-permute-done | bytes 524320 | tf_op jit(solution)/shard_map/while/body/eval_jaxpr/ppermute | solution.py:23
  165.0 9.3 %fusion.95 = (f32[16,64]{1,0:T(8,128)S(1)}, f32[16,64,256]{2,1,0:T(8,128)S(1)}) fusion(f32[256]{0:T(256)S(1)} %bitcast.215, bf16[22,67,256]{2,1,0:T(8,128)(2,1)S(1)} %get-tuple-element.534, f32[256]{0:T(256)S(1)} %bitcast.216, f32[256]{0:T(256)S(1)} %bitcast.217, f32[256]{0:T(256)S(1)} %bitcast.218, ...), kind=kLoop, calls=%fused_computation.158.clone.1 | loop fusion | flops 40369152 | bytes 23844864 | tf_op jit(solution)/shard_map/while/body/eval_jaxpr/reduce_sum | solution.py:27
  175.1 11.0 %convolution_add_fusion.2 = f32[1024,256]{1,0:T(8,128)S(1)} fusion(bf16[1024,256]{1,0:T(8,128)(2,1)} %get-tuple-element.638, bf16[1024,256]{1,0:T(8,128)(2,1)S(1)} %bitcast.182, bf16[256,1024]{1,0:T(8,128)(2,1)} %get-tuple-element.636, f32[1024]{0:T(1024)S(1)} %convert_element_type.1021, f32[256]{0:T(256)S(1)} %convert_element_type.1022), kind=kOutput, calls=%fused_computation.19.clone.1 | convolution fusion | flops 1143209984 | bytes 2626560 | tf_op jit(solution)/shard_map/while/body/eval_jaxpr/dot_general | solution.py:40
  188.5 8.6 %collective-permute-done.2 = bf16[16,64,256]{2,1,0:T(8,128)(2,1)S(1)} collective-permute-done((bf16[16,64,256]{2,1,0:T(8,128)(2,1)S(1)}, bf16[16,64,256]{2,1,0:T(8,128)(2,1)S(1)}, u32[]{:S(2)}, u32[]{:S(2)}) %collective-permute-start.2) | collective-permute-done | bytes 524320 | tf_op jit(solution)/shard_map/while/body/eval_jaxpr/ppermute | solution.py:23
  212.9 9.3 %fusion.95 = (f32[16,64]{1,0:T(8,128)S(1)}, f32[16,64,256]{2,1,0:T(8,128)S(1)}) fusion(f32[256]{0:T(256)S(1)} %bitcast.215, bf16[22,67,256]{2,1,0:T(8,128)(2,1)S(1)} %get-tuple-element.534, f32[256]{0:T(256)S(1)} %bitcast.216, f32[256]{0:T(256)S(1)} %bitcast.217, f32[256]{0:T(256)S(1)} %bitcast.218, ...), kind=kLoop, calls=%fused_computation.158.clone.1 | loop fusion | flops 40369152 | bytes 23844864 | tf_op jit(solution)/shard_map/while/body/eval_jaxpr/reduce_sum | solution.py:27
  223.0 11.0 %convolution_add_fusion.2 = f32[1024,256]{1,0:T(8,128)S(1)} fusion(bf16[1024,256]{1,0:T(8,128)(2,1)} %get-tuple-element.638, bf16[1024,256]{1,0:T(8,128)(2,1)S(1)} %bitcast.182, bf16[256,1024]{1,0:T(8,128)(2,1)} %get-tuple-element.636, f32[1024]{0:T(1024)S(1)} %convert_element_type.1021, f32[256]{0:T(256)S(1)} %convert_element_type.1022), kind=kOutput, calls=%fused_computation.19.clone.1 | convolution fusion | flops 1143209984 | bytes 2626560 | tf_op jit(solution)/shard_map/while/body/eval_jaxpr/dot_general | solution.py:40
  236.4 8.6 %collective-permute-done.2 = bf16[16,64,256]{2,1,0:T(8,128)(2,1)S(1)} collective-permute-done((bf16[16,64,256]{2,1,0:T(8,128)(2,1)S(1)}, bf16[16,64,256]{2,1,0:T(8,128)(2,1)S(1)}, u32[]{:S(2)}, u32[]{:S(2)}) %collective-permute-start.2) | collective-permute-done | bytes 524320 | tf_op jit(solution)/shard_map/while/body/eval_jaxpr/ppermute | solution.py:23
  260.5 9.3 %fusion.95 = (f32[16,64]{1,0:T(8,128)S(1)}, f32[16,64,256]{2,1,0:T(8,128)S(1)}) fusion(f32[256]{0:T(256)S(1)} %bitcast.215, bf16[22,67,256]{2,1,0:T(8,128)(2,1)S(1)} %get-tuple-element.534, f32[256]{0:T(256)S(1)} %bitcast.216, f32[256]{0:T(256)S(1)} %bitcast.217, f32[256]{0:T(256)S(1)} %bitcast.218, ...), kind=kLoop, calls=%fused_computation.158.clone.1 | loop fusion | flops 40369152 | bytes 23844864 | tf_op jit(solution)/shard_map/while/body/eval_jaxpr/reduce_sum | solution.py:27
  270.6 11.0 %convolution_add_fusion.2 = f32[1024,256]{1,0:T(8,128)S(1)} fusion(bf16[1024,256]{1,0:T(8,128)(2,1)} %get-tuple-element.638, bf16[1024,256]{1,0:T(8,128)(2,1)S(1)} %bitcast.182, bf16[256,1024]{1,0:T(8,128)(2,1)} %get-tuple-element.636, f32[1024]{0:T(1024)S(1)} %convert_element_type.1021, f32[256]{0:T(256)S(1)} %convert_element_type.1022), kind=kOutput, calls=%fused_computation.19.clone.1 | convolution fusion | flops 1143209984 | bytes 2626560 | tf_op jit(solution)/shard_map/while/body/eval_jaxpr/dot_general | solution.py:40
  284.0 8.6 %collective-permute-done.2 = bf16[16,64,256]{2,1,0:T(8,128)(2,1)S(1)} collective-permute-done((bf16[16,64,256]{2,1,0:T(8,128)(2,1)S(1)}, bf16[16,64,256]{2,1,0:T(8,128)(2,1)S(1)}, u32[]{:S(2)}, u32[]{:S(2)}) %collective-permute-start.2) | collective-permute-done | bytes 524320 | tf_op jit(solution)/shard_map/while/body/eval_jaxpr/ppermute | solution.py:23
  307.8 9.3 %fusion.95 = (f32[16,64]{1,0:T(8,128)S(1)}, f32[16,64,256]{2,1,0:T(8,128)S(1)}) fusion(f32[256]{0:T(256)S(1)} %bitcast.215, bf16[22,67,256]{2,1,0:T(8,128)(2,1)S(1)} %get-tuple-element.534, f32[256]{0:T(256)S(1)} %bitcast.216, f32[256]{0:T(256)S(1)} %bitcast.217, f32[256]{0:T(256)S(1)} %bitcast.218, ...), kind=kLoop, calls=%fused_computation.158.clone.1 | loop fusion | flops 40369152 | bytes 23844864 | tf_op jit(solution)/shard_map/while/body/eval_jaxpr/reduce_sum | solution.py:27
  317.9 11.0 %convolution_add_fusion.2 = f32[1024,256]{1,0:T(8,128)S(1)} fusion(bf16[1024,256]{1,0:T(8,128)(2,1)} %get-tuple-element.638, bf16[1024,256]{1,0:T(8,128)(2,1)S(1)} %bitcast.182, bf16[256,1024]{1,0:T(8,128)(2,1)} %get-tuple-element.636, f32[1024]{0:T(1024)S(1)} %convert_element_type.1021, f32[256]{0:T(256)S(1)} %convert_element_type.1022), kind=kOutput, calls=%fused_computation.19.clone.1 | convolution fusion | flops 1143209984 | bytes 2626560 | tf_op jit(solution)/shard_map/while/body/eval_jaxpr/dot_general | solution.py:40
  331.3 8.6 %collective-permute-done.2 = bf16[16,64,256]{2,1,0:T(8,128)(2,1)S(1)} collective-permute-done((bf16[16,64,256]{2,1,0:T(8,128)(2,1)S(1)}, bf16[16,64,256]{2,1,0:T(8,128)(2,1)S(1)}, u32[]{:S(2)}, u32[]{:S(2)}) %collective-permute-start.2) | collective-permute-done | bytes 524320 | tf_op jit(solution)/shard_map/while/body/eval_jaxpr/ppermute | solution.py:23
  354.8 9.3 %fusion.95 = (f32[16,64]{1,0:T(8,128)S(1)}, f32[16,64,256]{2,1,0:T(8,128)S(1)}) fusion(f32[256]{0:T(256)S(1)} %bitcast.215, bf16[22,67,256]{2,1,0:T(8,128)(2,1)S(1)} %get-tuple-element.534, f32[256]{0:T(256)S(1)} %bitcast.216, f32[256]{0:T(256)S(1)} %bitcast.217, f32[256]{0:T(256)S(1)} %bitcast.218, ...), kind=kLoop, calls=%fused_computation.158.clone.1 | loop fusion | flops 40369152 | bytes 23844864 | tf_op jit(solution)/shard_map/while/body/eval_jaxpr/reduce_sum | solution.py:27
  364.9 11.0 %convolution_add_fusion.2 = f32[1024,256]{1,0:T(8,128)S(1)} fusion(bf16[1024,256]{1,0:T(8,128)(2,1)} %get-tuple-element.638, bf16[1024,256]{1,0:T(8,128)(2,1)S(1)} %bitcast.182, bf16[256,1024]{1,0:T(8,128)(2,1)} %get-tuple-element.636, f32[1024]{0:T(1024)S(1)} %convert_element_type.1021, f32[256]{0:T(256)S(1)} %convert_element_type.1022), kind=kOutput, calls=%fused_computation.19.clone.1 | convolution fusion | flops 1143209984 | bytes 2626560 | tf_op jit(solution)/shard_map/while/body/eval_jaxpr/dot_general | solution.py:40
  378.4 8.6 %collective-permute-done.2 = bf16[16,64,256]{2,1,0:T(8,128)(2,1)S(1)} collective-permute-done((bf16[16,64,256]{2,1,0:T(8,128)(2,1)S(1)}, bf16[16,64,256]{2,1,0:T(8,128)(2,1)S(1)}, u32[]{:S(2)}, u32[]{:S(2)}) %collective-permute-start.2) | collective-permute-done | bytes 524320 | tf_op jit(solution)/shard_map/while/body/eval_jaxpr/ppermute | solution.py:23
  401.6 9.3 %fusion.95 = (f32[16,64]{1,0:T(8,128)S(1)}, f32[16,64,256]{2,1,0:T(8,128)S(1)}) fusion(f32[256]{0:T(256)S(1)} %bitcast.215, bf16[22,67,256]{2,1,0:T(8,128)(2,1)S(1)} %get-tuple-element.534, f32[256]{0:T(256)S(1)} %bitcast.216, f32[256]{0:T(256)S(1)} %bitcast.217, f32[256]{0:T(256)S(1)} %bitcast.218, ...), kind=kLoop, calls=%fused_computation.158.clone.1 | loop fusion | flops 40369152 | bytes 23844864 | tf_op jit(solution)/shard_map/while/body/eval_jaxpr/reduce_sum | solution.py:27
  411.6 11.0 %convolution_add_fusion.2 = f32[1024,256]{1,0:T(8,128)S(1)} fusion(bf16[1024,256]{1,0:T(8,128)(2,1)} %get-tuple-element.638, bf16[1024,256]{1,0:T(8,128)(2,1)S(1)} %bitcast.182, bf16[256,1024]{1,0:T(8,128)(2,1)} %get-tuple-element.636, f32[1024]{0:T(1024)S(1)} %convert_element_type.1021, f32[256]{0:T(256)S(1)} %convert_element_type.1022), kind=kOutput, calls=%fused_computation.19.clone.1 | convolution fusion | flops 1143209984 | bytes 2626560 | tf_op jit(solution)/shard_map/while/body/eval_jaxpr/dot_general | solution.py:40
  425.1 8.6 %collective-permute-done.2 = bf16[16,64,256]{2,1,0:T(8,128)(2,1)S(1)} collective-permute-done((bf16[16,64,256]{2,1,0:T(8,128)(2,1)S(1)}, bf16[16,64,256]{2,1,0:T(8,128)(2,1)S(1)}, u32[]{:S(2)}, u32[]{:S(2)}) %collective-permute-start.2) | collective-permute-done | bytes 524320 | tf_op jit(solution)/shard_map/while/body/eval_jaxpr/ppermute | solution.py:23
  448.0 9.3 %fusion.95 = (f32[16,64]{1,0:T(8,128)S(1)}, f32[16,64,256]{2,1,0:T(8,128)S(1)}) fusion(f32[256]{0:T(256)S(1)} %bitcast.215, bf16[22,67,256]{2,1,0:T(8,128)(2,1)S(1)} %get-tuple-element.534, f32[256]{0:T(256)S(1)} %bitcast.216, f32[256]{0:T(256)S(1)} %bitcast.217, f32[256]{0:T(256)S(1)} %bitcast.218, ...), kind=kLoop, calls=%fused_computation.158.clone.1 | loop fusion | flops 40369152 | bytes 23844864 | tf_op jit(solution)/shard_map/while/body/eval_jaxpr/reduce_sum | solution.py:27
  458.1 11.0 %convolution_add_fusion.2 = f32[1024,256]{1,0:T(8,128)S(1)} fusion(bf16[1024,256]{1,0:T(8,128)(2,1)} %get-tuple-element.638, bf16[1024,256]{1,0:T(8,128)(2,1)S(1)} %bitcast.182, bf16[256,1024]{1,0:T(8,128)(2,1)} %get-tuple-element.636, f32[1024]{0:T(1024)S(1)} %convert_element_type.1021, f32[256]{0:T(256)S(1)} %convert_element_type.1022), kind=kOutput, calls=%fused_computation.19.clone.1 | convolution fusion | flops 1143209984 | bytes 2626560 | tf_op jit(solution)/shard_map/while/body/eval_jaxpr/dot_general | solution.py:40
  494.1 9.3 %fusion.95 = (f32[16,64]{1,0:T(8,128)S(1)}, f32[16,64,256]{2,1,0:T(8,128)S(1)}) fusion(f32[256]{0:T(256)S(1)} %bitcast.215, bf16[22,67,256]{2,1,0:T(8,128)(2,1)S(1)} %get-tuple-element.534, f32[256]{0:T(256)S(1)} %bitcast.216, f32[256]{0:T(256)S(1)} %bitcast.217, f32[256]{0:T(256)S(1)} %bitcast.218, ...), kind=kLoop, calls=%fused_computation.158.clone.1 | loop fusion | flops 40369152 | bytes 23844864 | tf_op jit(solution)/shard_map/while/body/eval_jaxpr/reduce_sum | solution.py:27
  504.2 11.0 %convolution_add_fusion.2 = f32[1024,256]{1,0:T(8,128)S(1)} fusion(bf16[1024,256]{1,0:T(8,128)(2,1)} %get-tuple-element.638, bf16[1024,256]{1,0:T(8,128)(2,1)S(1)} %bitcast.182, bf16[256,1024]{1,0:T(8,128)(2,1)} %get-tuple-element.636, f32[1024]{0:T(1024)S(1)} %convert_element_type.1021, f32[256]{0:T(256)S(1)} %convert_element_type.1022), kind=kOutput, calls=%fused_computation.19.clone.1 | convolution fusion | flops 1143209984 | bytes 2626560 | tf_op jit(solution)/shard_map/while/body/eval_jaxpr/dot_general | solution.py:40
  (254 shorter events, 223.5 us)
Async XLA Ops:
  8.2 7.3 %collective-permute-start = (bf16[3,64,256]{2,1,0:T(8,128)(2,1)S(1)}, bf16[3,64,256]{2,1,0:T(8,128)(2,1)S(1)}, u32[]{:S(2)}, u32[]{:S(2)}) collective-permute-start(bf16[3,64,256]{2,1,0:T(8,128)(2,1)S(1)} %get-tuple-element.532), channel_id=1, source_target_pairs={{4,0},{8,4},{12,8},{16,12},{20,16},{24,20},{28,24},{32,28},{36,32}... | collective-permute-start | bytes 294920 | tf_op jit(solution)/shard_map/while/body/eval_jaxpr/ppermute | solution.py:15
  10.8 8.0 %collective-permute-start.1 = (bf16[3,64,256]{2,1,0:T(8,128)(2,1)S(1)}, bf16[3,64,256]{2,1,0:T(8,128)(2,1)S(1)}, u32[]{:S(2)}, u32[]{:S(2)}) collective-permute-start(bf16[3,64,256]{2,1,0:T(8,128)(2,1)S(1)} %get-tuple-element.533), channel_id=1, source_target_pairs={{0,4},{4,8},{8,12},{12,16},{16,20},{20,24},{24,28},{28,32},{32,36}... | collective-permute-start | bytes 294920 | tf_op jit(solution)/shard_map/while/body/eval_jaxpr/ppermute | solution.py:12
  41.5 9.9 %collective-permute-start.2 = (bf16[16,64,256]{2,1,0:T(8,128)(2,1)S(1)}, bf16[16,64,256]{2,1,0:T(8,128)(2,1)S(1)}, u32[]{:S(2)}, u32[]{:S(2)}) collective-permute-start(bf16[16,64,256]{2,1,0:T(8,128)(2,1)S(1)} %get-tuple-element.586), channel_id=1, source_target_pairs={{0,1},{1,2},{2,3},{4,5},{5,6},{6,7},{8,9},{9,10},{10,11},{12,13},{... | collective-permute-start | bytes 1572872 | tf_op jit(solution)/shard_map/while/body/eval_jaxpr/ppermute | solution.py:23
  52.8 11.6 %collective-permute-start = (bf16[3,64,256]{2,1,0:T(8,128)(2,1)S(1)}, bf16[3,64,256]{2,1,0:T(8,128)(2,1)S(1)}, u32[]{:S(2)}, u32[]{:S(2)}) collective-permute-start(bf16[3,64,256]{2,1,0:T(8,128)(2,1)S(1)} %get-tuple-element.532), channel_id=1, source_target_pairs={{4,0},{8,4},{12,8},{16,12},{20,16},{24,20},{28,24},{32,28},{36,32}... | collective-permute-start | bytes 294920 | tf_op jit(solution)/shard_map/while/body/eval_jaxpr/ppermute | solution.py:15
  61.2 6.7 %collective-permute-start.1 = (bf16[3,64,256]{2,1,0:T(8,128)(2,1)S(1)}, bf16[3,64,256]{2,1,0:T(8,128)(2,1)S(1)}, u32[]{:S(2)}, u32[]{:S(2)}) collective-permute-start(bf16[3,64,256]{2,1,0:T(8,128)(2,1)S(1)} %get-tuple-element.533), channel_id=1, source_target_pairs={{0,4},{4,8},{8,12},{12,16},{16,20},{20,24},{24,28},{28,32},{32,36}... | collective-permute-start | bytes 294920 | tf_op jit(solution)/shard_map/while/body/eval_jaxpr/ppermute | solution.py:12
  90.6 9.9 %collective-permute-start.2 = (bf16[16,64,256]{2,1,0:T(8,128)(2,1)S(1)}, bf16[16,64,256]{2,1,0:T(8,128)(2,1)S(1)}, u32[]{:S(2)}, u32[]{:S(2)}) collective-permute-start(bf16[16,64,256]{2,1,0:T(8,128)(2,1)S(1)} %get-tuple-element.586), channel_id=1, source_target_pairs={{0,1},{1,2},{2,3},{4,5},{5,6},{6,7},{8,9},{9,10},{10,11},{12,13},{... | collective-permute-start | bytes 1572872 | tf_op jit(solution)/shard_map/while/body/eval_jaxpr/ppermute | solution.py:23
  101.9 11.6 %collective-permute-start = (bf16[3,64,256]{2,1,0:T(8,128)(2,1)S(1)}, bf16[3,64,256]{2,1,0:T(8,128)(2,1)S(1)}, u32[]{:S(2)}, u32[]{:S(2)}) collective-permute-start(bf16[3,64,256]{2,1,0:T(8,128)(2,1)S(1)} %get-tuple-element.532), channel_id=1, source_target_pairs={{4,0},{8,4},{12,8},{16,12},{20,16},{24,20},{28,24},{32,28},{36,32}... | collective-permute-start | bytes 294920 | tf_op jit(solution)/shard_map/while/body/eval_jaxpr/ppermute | solution.py:15
  110.3 6.1 %collective-permute-start.1 = (bf16[3,64,256]{2,1,0:T(8,128)(2,1)S(1)}, bf16[3,64,256]{2,1,0:T(8,128)(2,1)S(1)}, u32[]{:S(2)}, u32[]{:S(2)}) collective-permute-start(bf16[3,64,256]{2,1,0:T(8,128)(2,1)S(1)} %get-tuple-element.533), channel_id=1, source_target_pairs={{0,4},{4,8},{8,12},{12,16},{16,20},{20,24},{24,28},{28,32},{32,36}... | collective-permute-start | bytes 294920 | tf_op jit(solution)/shard_map/while/body/eval_jaxpr/ppermute | solution.py:12
  139.1 9.9 %collective-permute-start.2 = (bf16[16,64,256]{2,1,0:T(8,128)(2,1)S(1)}, bf16[16,64,256]{2,1,0:T(8,128)(2,1)S(1)}, u32[]{:S(2)}, u32[]{:S(2)}) collective-permute-start(bf16[16,64,256]{2,1,0:T(8,128)(2,1)S(1)} %get-tuple-element.586), channel_id=1, source_target_pairs={{0,1},{1,2},{2,3},{4,5},{5,6},{6,7},{8,9},{9,10},{10,11},{12,13},{... | collective-permute-start | bytes 1572872 | tf_op jit(solution)/shard_map/while/body/eval_jaxpr/ppermute | solution.py:23
  150.4 11.6 %collective-permute-start = (bf16[3,64,256]{2,1,0:T(8,128)(2,1)S(1)}, bf16[3,64,256]{2,1,0:T(8,128)(2,1)S(1)}, u32[]{:S(2)}, u32[]{:S(2)}) collective-permute-start(bf16[3,64,256]{2,1,0:T(8,128)(2,1)S(1)} %get-tuple-element.532), channel_id=1, source_target_pairs={{4,0},{8,4},{12,8},{16,12},{20,16},{24,20},{28,24},{32,28},{36,32}... | collective-permute-start | bytes 294920 | tf_op jit(solution)/shard_map/while/body/eval_jaxpr/ppermute | solution.py:15
  158.8 5.8 %collective-permute-start.1 = (bf16[3,64,256]{2,1,0:T(8,128)(2,1)S(1)}, bf16[3,64,256]{2,1,0:T(8,128)(2,1)S(1)}, u32[]{:S(2)}, u32[]{:S(2)}) collective-permute-start(bf16[3,64,256]{2,1,0:T(8,128)(2,1)S(1)} %get-tuple-element.533), channel_id=1, source_target_pairs={{0,4},{4,8},{8,12},{12,16},{16,20},{20,24},{24,28},{28,32},{32,36}... | collective-permute-start | bytes 294920 | tf_op jit(solution)/shard_map/while/body/eval_jaxpr/ppermute | solution.py:12
  187.3 9.9 %collective-permute-start.2 = (bf16[16,64,256]{2,1,0:T(8,128)(2,1)S(1)}, bf16[16,64,256]{2,1,0:T(8,128)(2,1)S(1)}, u32[]{:S(2)}, u32[]{:S(2)}) collective-permute-start(bf16[16,64,256]{2,1,0:T(8,128)(2,1)S(1)} %get-tuple-element.586), channel_id=1, source_target_pairs={{0,1},{1,2},{2,3},{4,5},{5,6},{6,7},{8,9},{9,10},{10,11},{12,13},{... | collective-permute-start | bytes 1572872 | tf_op jit(solution)/shard_map/while/body/eval_jaxpr/ppermute | solution.py:23
  198.6 11.6 %collective-permute-start = (bf16[3,64,256]{2,1,0:T(8,128)(2,1)S(1)}, bf16[3,64,256]{2,1,0:T(8,128)(2,1)S(1)}, u32[]{:S(2)}, u32[]{:S(2)}) collective-permute-start(bf16[3,64,256]{2,1,0:T(8,128)(2,1)S(1)} %get-tuple-element.532), channel_id=1, source_target_pairs={{4,0},{8,4},{12,8},{16,12},{20,16},{24,20},{28,24},{32,28},{36,32}... | collective-permute-start | bytes 294920 | tf_op jit(solution)/shard_map/while/body/eval_jaxpr/ppermute | solution.py:15
  207.0 5.5 %collective-permute-start.1 = (bf16[3,64,256]{2,1,0:T(8,128)(2,1)S(1)}, bf16[3,64,256]{2,1,0:T(8,128)(2,1)S(1)}, u32[]{:S(2)}, u32[]{:S(2)}) collective-permute-start(bf16[3,64,256]{2,1,0:T(8,128)(2,1)S(1)} %get-tuple-element.533), channel_id=1, source_target_pairs={{0,4},{4,8},{8,12},{12,16},{16,20},{20,24},{24,28},{28,32},{32,36}... | collective-permute-start | bytes 294920 | tf_op jit(solution)/shard_map/while/body/eval_jaxpr/ppermute | solution.py:12
  235.1 9.9 %collective-permute-start.2 = (bf16[16,64,256]{2,1,0:T(8,128)(2,1)S(1)}, bf16[16,64,256]{2,1,0:T(8,128)(2,1)S(1)}, u32[]{:S(2)}, u32[]{:S(2)}) collective-permute-start(bf16[16,64,256]{2,1,0:T(8,128)(2,1)S(1)} %get-tuple-element.586), channel_id=1, source_target_pairs={{0,1},{1,2},{2,3},{4,5},{5,6},{6,7},{8,9},{9,10},{10,11},{12,13},{... | collective-permute-start | bytes 1572872 | tf_op jit(solution)/shard_map/while/body/eval_jaxpr/ppermute | solution.py:23
  246.5 11.6 %collective-permute-start = (bf16[3,64,256]{2,1,0:T(8,128)(2,1)S(1)}, bf16[3,64,256]{2,1,0:T(8,128)(2,1)S(1)}, u32[]{:S(2)}, u32[]{:S(2)}) collective-permute-start(bf16[3,64,256]{2,1,0:T(8,128)(2,1)S(1)} %get-tuple-element.532), channel_id=1, source_target_pairs={{4,0},{8,4},{12,8},{16,12},{20,16},{24,20},{28,24},{32,28},{36,32}... | collective-permute-start | bytes 294920 | tf_op jit(solution)/shard_map/while/body/eval_jaxpr/ppermute | solution.py:15
  254.9 5.2 collective-permute-start.1
  282.7 9.9 %collective-permute-start.2 = (bf16[16,64,256]{2,1,0:T(8,128)(2,1)S(1)}, bf16[16,64,256]{2,1,0:T(8,128)(2,1)S(1)}, u32[]{:S(2)}, u32[]{:S(2)}) collective-permute-start(bf16[16,64,256]{2,1,0:T(8,128)(2,1)S(1)} %get-tuple-element.586), channel_id=1, source_target_pairs={{0,1},{1,2},{2,3},{4,5},{5,6},{6,7},{8,9},{9,10},{10,11},{12,13},{... | collective-permute-start | bytes 1572872 | tf_op jit(solution)/shard_map/while/body/eval_jaxpr/ppermute | solution.py:23
  294.1 11.6 %collective-permute-start = (bf16[3,64,256]{2,1,0:T(8,128)(2,1)S(1)}, bf16[3,64,256]{2,1,0:T(8,128)(2,1)S(1)}, u32[]{:S(2)}, u32[]{:S(2)}) collective-permute-start(bf16[3,64,256]{2,1,0:T(8,128)(2,1)S(1)} %get-tuple-element.532), channel_id=1, source_target_pairs={{4,0},{8,4},{12,8},{16,12},{20,16},{24,20},{28,24},{32,28},{36,32}... | collective-permute-start | bytes 294920 | tf_op jit(solution)/shard_map/while/body/eval_jaxpr/ppermute | solution.py:15
  302.5 4.9 collective-permute-start.1
  330.1 9.9 %collective-permute-start.2 = (bf16[16,64,256]{2,1,0:T(8,128)(2,1)S(1)}, bf16[16,64,256]{2,1,0:T(8,128)(2,1)S(1)}, u32[]{:S(2)}, u32[]{:S(2)}) collective-permute-start(bf16[16,64,256]{2,1,0:T(8,128)(2,1)S(1)} %get-tuple-element.586), channel_id=1, source_target_pairs={{0,1},{1,2},{2,3},{4,5},{5,6},{6,7},{8,9},{9,10},{10,11},{12,13},{... | collective-permute-start | bytes 1572872 | tf_op jit(solution)/shard_map/while/body/eval_jaxpr/ppermute | solution.py:23
  341.4 11.6 %collective-permute-start = (bf16[3,64,256]{2,1,0:T(8,128)(2,1)S(1)}, bf16[3,64,256]{2,1,0:T(8,128)(2,1)S(1)}, u32[]{:S(2)}, u32[]{:S(2)}) collective-permute-start(bf16[3,64,256]{2,1,0:T(8,128)(2,1)S(1)} %get-tuple-element.532), channel_id=1, source_target_pairs={{4,0},{8,4},{12,8},{16,12},{20,16},{24,20},{28,24},{32,28},{36,32}... | collective-permute-start | bytes 294920 | tf_op jit(solution)/shard_map/while/body/eval_jaxpr/ppermute | solution.py:15
  349.8 4.6 collective-permute-start.1
  377.1 9.9 %collective-permute-start.2 = (bf16[16,64,256]{2,1,0:T(8,128)(2,1)S(1)}, bf16[16,64,256]{2,1,0:T(8,128)(2,1)S(1)}, u32[]{:S(2)}, u32[]{:S(2)}) collective-permute-start(bf16[16,64,256]{2,1,0:T(8,128)(2,1)S(1)} %get-tuple-element.586), channel_id=1, source_target_pairs={{0,1},{1,2},{2,3},{4,5},{5,6},{6,7},{8,9},{9,10},{10,11},{12,13},{... | collective-permute-start | bytes 1572872 | tf_op jit(solution)/shard_map/while/body/eval_jaxpr/ppermute | solution.py:23
  388.4 11.6 %collective-permute-start = (bf16[3,64,256]{2,1,0:T(8,128)(2,1)S(1)}, bf16[3,64,256]{2,1,0:T(8,128)(2,1)S(1)}, u32[]{:S(2)}, u32[]{:S(2)}) collective-permute-start(bf16[3,64,256]{2,1,0:T(8,128)(2,1)S(1)} %get-tuple-element.532), channel_id=1, source_target_pairs={{4,0},{8,4},{12,8},{16,12},{20,16},{24,20},{28,24},{32,28},{36,32}... | collective-permute-start | bytes 294920 | tf_op jit(solution)/shard_map/while/body/eval_jaxpr/ppermute | solution.py:15
  396.8 4.3 collective-permute-start.1
  423.8 9.9 %collective-permute-start.2 = (bf16[16,64,256]{2,1,0:T(8,128)(2,1)S(1)}, bf16[16,64,256]{2,1,0:T(8,128)(2,1)S(1)}, u32[]{:S(2)}, u32[]{:S(2)}) collective-permute-start(bf16[16,64,256]{2,1,0:T(8,128)(2,1)S(1)} %get-tuple-element.586), channel_id=1, source_target_pairs={{0,1},{1,2},{2,3},{4,5},{5,6},{6,7},{8,9},{9,10},{10,11},{12,13},{... | collective-permute-start | bytes 1572872 | tf_op jit(solution)/shard_map/while/body/eval_jaxpr/ppermute | solution.py:23
  435.1 11.6 %collective-permute-start = (bf16[3,64,256]{2,1,0:T(8,128)(2,1)S(1)}, bf16[3,64,256]{2,1,0:T(8,128)(2,1)S(1)}, u32[]{:S(2)}, u32[]{:S(2)}) collective-permute-start(bf16[3,64,256]{2,1,0:T(8,128)(2,1)S(1)} %get-tuple-element.532), channel_id=1, source_target_pairs={{4,0},{8,4},{12,8},{16,12},{20,16},{24,20},{28,24},{32,28},{36,32}... | collective-permute-start | bytes 294920 | tf_op jit(solution)/shard_map/while/body/eval_jaxpr/ppermute | solution.py:15
  443.5 4.0 collective-permute-start.1
  470.2 9.9 %collective-permute-start.2 = (bf16[16,64,256]{2,1,0:T(8,128)(2,1)S(1)}, bf16[16,64,256]{2,1,0:T(8,128)(2,1)S(1)}, u32[]{:S(2)}, u32[]{:S(2)}) collective-permute-start(bf16[16,64,256]{2,1,0:T(8,128)(2,1)S(1)} %get-tuple-element.586), channel_id=1, source_target_pairs={{0,1},{1,2},{2,3},{4,5},{5,6},{6,7},{8,9},{9,10},{10,11},{12,13},{... | collective-permute-start | bytes 1572872 | tf_op jit(solution)/shard_map/while/body/eval_jaxpr/ppermute | solution.py:23
  481.5 11.6 %collective-permute-start = (bf16[3,64,256]{2,1,0:T(8,128)(2,1)S(1)}, bf16[3,64,256]{2,1,0:T(8,128)(2,1)S(1)}, u32[]{:S(2)}, u32[]{:S(2)}) collective-permute-start(bf16[3,64,256]{2,1,0:T(8,128)(2,1)S(1)} %get-tuple-element.532), channel_id=1, source_target_pairs={{4,0},{8,4},{12,8},{16,12},{20,16},{24,20},{28,24},{32,28},{36,32}... | collective-permute-start | bytes 294920 | tf_op jit(solution)/shard_map/while/body/eval_jaxpr/ppermute | solution.py:15
  516.3 9.9 %collective-permute-start.2 = (bf16[16,64,256]{2,1,0:T(8,128)(2,1)S(1)}, bf16[16,64,256]{2,1,0:T(8,128)(2,1)S(1)}, u32[]{:S(2)}, u32[]{:S(2)}) collective-permute-start(bf16[16,64,256]{2,1,0:T(8,128)(2,1)S(1)} %get-tuple-element.586), channel_id=1, source_target_pairs={{0,1},{1,2},{2,3},{4,5},{5,6},{6,7},{8,9},{9,10},{10,11},{12,13},{... | collective-permute-start | bytes 1572872 | tf_op jit(solution)/shard_map/while/body/eval_jaxpr/ppermute | solution.py:23
  (2 other events, 10.5 us)
where the time goes:
time: 535 us; the launch traced here: 526 us
  other arithmetic  149 us (28%)
  starting transfers between devices  123 us (23%)
  matrix products  121 us (23%)
  waiting for transfers between devices  117 us (22%)
  local copies, waits for them, and re-layouts  14.7 us (3%)
    dot_general x11, matrix products, pointwise(): jnp.dot(hidden, down_w, preferred_element_type=jnp.float32)  121 us
    reduce_sum x11, other arithmetic, layer_norm(): centre = jnp.mean(summed, axis=-1, keepdims=True)  102 us
    ppermute x11, waiting for transfers between devices, passed_along(): return lax.ppermute(array, axis, pairs)  94.8 us
    ppermute x11, starting transfers between devices, extended(): lax.ppermute(lax.slice_in_dim(block, 0, width, axis=dim), axis, backward)  86.6 us
    ppermute x11, starting transfers between devices, extended(): lax.ppermute(lax.slice_in_dim(block, block.shape[dim] - width, None, axis...  22.6 us
    ppermute x11, waiting for transfers between devices, extended(): lax.ppermute(lax.slice_in_dim(block, block.shape[dim] - width, None, axis...  22 us
    select_n x11, other arithmetic, tick(): current = jnp.where(segment_no == 0, fresh, incoming)  15 us
    ppermute x11, starting transfers between devices, passed_along(): return lax.ppermute(array, axis, pairs)  14.1 us
  transfers between devices with their start and end apart: 33, of which 22 were waited for; matrix products, arithmetic and copies ran while one was open for 2% of the time, Pallas kernels for 0%

commit v1 on v0

v1 whole, which is shorter than its diff:
```python
import jax
import jax.numpy as jnp
from jax import lax
from jax.experimental import pallas as pl
from jax.experimental.pallas import tpu as pltpu
from jax.sharding import PartitionSpec as P

BF, F32 = jnp.bfloat16, jnp.float32
MESH = pl.DeviceIdType.MESH
KS, REACH = 7, 3
R, W, C, HID = 16, 64, 256, 1024
BLOCKS, DATES, BANDS = 4, 2, 64
PIECES = 8
UPR, DNR = C // PIECES, HID // PIECES
CH = 4
NCH = R // CH


def tree(p):
    return ((p[0] + p[1]) + (p[2] + p[3])) + ((p[4] + p[5]) + p[6])


def conv_row(state, taps, sp, normed, i):
    xs = [state[i + a].reshape(W // 8, 8, C) for a in range(KS)]
    acc = None
    for b in range(KS):
        t = tree([xs[a] * taps[a * KS + b][None] for a in range(KS)])
        t = t.astype(F32).reshape(W, C)
        if b != REACH:
            t = pltpu.roll(t, (REACH - b) % W, 0)
        acc = t if acc is None else acc + t
    summed = acc + sp[0:1, 0:C]
    mean = jnp.sum(summed, -1, keepdims=True) * (1.0 / C)
    dev = summed - mean
    var = jnp.sum(dev * dev, -1, keepdims=True) * (1.0 / C)
    out = dev * lax.rsqrt(var + 1e-6) * sp[1:2, 0:C] + sp[2:3, 0:C]
    normed[pl.ds(pl.multiple_of(i * W, W), W), :] = out.astype(BF)


def mlp_chunk(normed, state, result, mask, up, dn, sp, hid, ck):
    m = CH * W
    r0 = pl.multiple_of(ck * m, m)
    n = normed[pl.ds(r0, m), :]
    for j in range(4):
        js = slice(j * 256, (j + 1) * 256)
        h = jnp.dot(n, up[:, js], preferred_element_type=F32) + sp[4:5, js]
        v = h.astype(BF)
        e = lax.erf(v * jnp.asarray(0.7071067811865476, BF))
        hid[:, js] = v + v * e
    u = jnp.dot(hid[...], dn[...], preferred_element_type=F32) * 0.5 + sp[3:4, 0:C]
    st = state[pl.ds(ck * CH + REACH, CH)].reshape(m, C).astype(F32)
    mk = mask[pl.ds(r0, m), :]
    o = (st + u) * jnp.concatenate([mk, mk], axis=1)
    result[pl.ds(ck * CH + REACH, CH)] = o.astype(BF).reshape(CH, W, C)


def kernel(fields, land, ck, cb, ng, ns, up, ub, dn, db, out,
           S, WU, WD, CK, SP, TP, N, H, MK,
           f_sem, own_sem, y_send, k_send, k_recv, w_recv, x_send, c_send,
           h_send, h_recv, o_send, o_recv, l_sem):
    band, q = lax.axis_index("band"), lax.axis_index("segment")
    core = lax.rem(band, 2)
    xpos = band // 16
    sib = band + 1 - 2 * core
    other = jnp.where(core == 0, band - 1, band + 1)
    has_prev, has_next = band > 0, band < BANDS - 1
    has_other = jnp.logical_and(other >= 0, other < BANDS)
    mine = 2 * xpos + core

    def at(b, s):
        return {"band": b, "segment": s}

    def x_band(k):
        return lax.rem(band + 16 * k, BANDS)

    def seg(r):
        return lax.rem(q + r, BLOCKS)

    barrier = pltpu.get_barrier_semaphore()

    def greet(b, s):
        pl.semaphore_signal(barrier, inc=1, device_id=at(b, s), device_id_type=MESH)

    for r in (1, 2, 3):
        greet(band, seg(r))
    for k in (1, 2, 3):
        greet(x_band(k), q)
    greet(sib, q)

    @pl.when(has_other)
    def _():
        greet(other, q)

    def field_copy(d):
        return pltpu.make_async_copy(
            fields.at[DATES * q + d], S.at[d, 0, pl.ds(REACH, R)], f_sem.at[d])

    field_copy(0).start()
    field_copy(1).start()
    own_up = pltpu.make_async_copy(up.at[0], WU.at[q], own_sem.at[0])
    own_dn = pltpu.make_async_copy(dn.at[0], WD.at[q], own_sem.at[1])
    own_up.start()
    own_dn.start()

    CK[q] = ck[0]
    SP[q, 0:1, 0:C] = cb[...].astype(F32)
    SP[q, 1:2, 0:C] = ng[...].astype(F32)
    SP[q, 2:3, 0:C] = ns[...].astype(F32)
    SP[q, 3:4, 0:C] = db[...].astype(F32)
    SP[q, 4:5, :] = ub[...].astype(F32)

    eye = (lax.broadcasted_iota(jnp.int32, (W, W), 0)
           == lax.broadcasted_iota(jnp.int32, (W, W), 1))

    @pl.loop(0, R)
    def _(i):
        row = jnp.broadcast_to(land[pl.ds(i, 1), :].astype(F32), (W, W))
        col = jnp.sum(jnp.where(eye, row, 0.0), -1, keepdims=True)
        MK[pl.ds(pl.multiple_of(i * W, W), W), :] = jnp.broadcast_to(col, (W, 128))

    edge = jnp.zeros((REACH, W, C), BF)

    @pl.when(jnp.logical_not(has_prev))
    def _():
        @pl.loop(0, DATES * BLOCKS)
        def _(t):
            S[t // BLOCKS, lax.rem(t, BLOCKS), 0:REACH] = edge

    @pl.when(jnp.logical_not(has_next))
    def _():
        @pl.loop(0, DATES * BLOCKS)
        def _(t):
            S[t // BLOCKS, lax.rem(t, BLOCKS), R + REACH:R + 2 * REACH] = edge

    pl.semaphore_wait(barrier, 7 + has_other.astype(jnp.int32))

    def k_copies(r, s):
        return (
            pltpu.make_async_remote_copy(
                CK.at[s], CK.at[s], k_send.at[r - 1, 0], k_recv.at[s, 0],
                device_id=at(band, seg(r)), device_id_type=MESH),
            pltpu.make_async_remote_copy(
                SP.at[s], SP.at[s], k_send.at[r - 1, 1], k_recv.at[s, 1],
                device_id=at(band, seg(r)), device_id_type=MESH))

    def part(ref, s, p, w):
        n = (UPR, DNR)[w]
        return ref.at[s, pl.ds(pl.multiple_of(p * n, n), n)]

    def y_copy(r, w):
        return pltpu.make_async_remote_copy(
            part((up, dn)[w], 0, mine, w), part((WU, WD)[w], q, mine, w),
            y_send.at[r - 1, w], w_recv.at[q, mine, w],
            device_id=at(band, seg(r)), device_id_type=MESH)

    def w_copy(s, p, w, b, sem):
        ref = (WU, WD)[w]
        return pltpu.make_async_remote_copy(
            part(ref, s, p, w), part(ref, s, p, w), sem, w_recv.at[s, p, w],
            device_id=at(b, q), device_id_type=MESH)

    def x_copy(s, k, w):
        return w_copy(s, mine, w, x_band(k), x_send.at[s, k - 1, w])

    def c_copy(s, k, w):
        p = 2 * lax.rem(xpos + k, 4) + core
        return w_copy(s, p, w, sib, c_send.at[s, k, w])

    for r in (1, 3, 2):
        for c in k_copies(r, q):
            c.start()
    for w in (0, 1):
        for r in (1, 3, 2):
            y_copy(r, w).start()

    def stage_x(s):
        @pl.when(q != s)
        def _():
            for w in (0, 1):
                c_copy(s, 0, w).wait_recv()
                for k in (1, 3, 2):
                    x_copy(s, k, w).start()
                c_copy(s, 0, w).start()

    def stage_c(s):
        @pl.when(q != s)
        def _():
            for w in (0, 1):
                for k in (1, 3, 2):
                    c_copy(s, k, w).wait_recv()
                    c_copy(s, k, w).start()

    def stage_f(s):
        @pl.when(q != s)
        def _():
            for w in (0, 1):
                for k in range(4):
                    p = 2 * k + 1 - core
                    w_copy(s, p, w, sib, c_send.at[s, k, w]).wait_recv()

        @pl.when(q == s)
        def _():
            own_up.wait()
            own_dn.wait()

    def halo(d, s, side):
        src = pl.ds(REACH, REACH) if side == 0 else pl.ds(R, REACH)
        dst = pl.ds(R + REACH, REACH) if side == 0 else pl.ds(0, REACH)
        to = band - 1 if side == 0 else band + 1
        return pltpu.make_async_remote_copy(
            S.at[d, s, src], S.at[d, s, dst], h_send.at[d, s, side], h_recv.at[d, s, side],
            device_id=at(to, q), device_id_type=MESH)

    def halo_start(d, s):
        @pl.when(has_prev)
        def _():
            halo(d, s, 0).start()

        @pl.when(has_next)
        def _():
            halo(d, s, 1).start()

    def halo_wait(d, s):
        @pl.when(has_next)
        def _():
            halo(d, s, 0).wait_recv()

        @pl.when(has_prev)
        def _():
            halo(d, s, 1).wait_recv()

    def halo_done(d, s):
        @pl.when(has_prev)
        def _():
            halo(d, s, 0).wait_send()

        @pl.when(has_next)
        def _():
            halo(d, s, 1).wait_send()

    for d in range(DATES):
        field_copy(d).wait()

        @pl.loop(0, R)
        def _(i):
            m = MK[pl.ds(pl.multiple_of(i * W, W), W), :]
            x = S[d, 0, i + REACH].astype(F32) * jnp.concatenate([m, m], axis=1)
            S[d, 0, i + REACH] = x.astype(BF)

        halo_start(d, 0)

    def rows(ref, ck):
        return ref.at[pl.ds(ck * CH, CH)]

    def o_copy(d, s, ck):
        return pltpu.make_async_remote_copy(
            S.at[d, s + 1, pl.ds(REACH + ck * CH, CH)],
            out.at[0, DATES * q + d, pl.ds(ck * CH, CH)],
            o_send.at[d, s, ck], o_recv.at[DATES * q + d, ck],
            device_id=at(band, s), device_id_type=MESH)

    def l_copy(d, s, ck):
        return pltpu.make_async_copy(
            S.at[d, s + 1, pl.ds(REACH + ck * CH, CH)],
            out.at[0, DATES * q + d, pl.ds(ck * CH, CH)], l_sem.at[d, ck])

    def send_out(d, s, ck):
        @pl.when(q != s)
        def _():
            o_copy(d, s, ck).start()

        @pl.when(q == s)
        def _():
            l_copy(d, s, ck).start()

    def order(t):
        return jnp.where(t == 1, NCH - 1, jnp.where(t > 1, t - 1, 0))

    @pl.loop(0, DATES * BLOCKS)
    def _(unit):
        d, s = unit // BLOCKS, lax.rem(unit, BLOCKS)
        state, result = S.at[d, s], S.at[d, s + 1]
        taps, sp, wu, wd = TP.at[s], SP.at[s], WU.at[s], WD.at[s]

        @pl.when(d == 0)
        def _():
            @pl.when(q != s)
            def _():
                for w in (0, 1):
                    pltpu.make_async_remote_copy(
                        (CK, SP)[w].at[s], (CK, SP)[w].at[s], k_send.at[0, w], k_recv.at[s, w],
                        device_id=at(band, seg(1)), device_id_type=MESH).wait_recv()

            @pl.loop(0, KS)
            def _(a):
                line = CK[s, a].astype(F32)
                for b in range(KS):
                    taps[a * KS + b] = jnp.broadcast_to(line[b:b + 1], (8, C)).astype(BF)

        @pl.loop(0, 5)
        def _(t):
            conv_row(state, taps, sp, N, 2 * t + 3)
            conv_row(state, taps, sp, N, 2 * t + 4)

        halo_wait(d, s)

        @pl.loop(0, 3)
        def _(t):
            conv_row(state, taps, sp, N, t)
            conv_row(state, taps, sp, N, t + 13)

        @pl.when(d == 0)
        def _():
            @pl.when(s == 0)
            def _():
                stage_x(0)
                stage_c(0)
            stage_f(s)

            @pl.when(s < BLOCKS - 1)
            def _():
                stage_x(s + 1)

        @pl.loop(0, NCH)
        def _(t):
            mlp_chunk(N, state, result, MK, wu, wd, sp, H, order(t))

            @pl.when(jnp.logical_and(t == 1, s < BLOCKS - 1))
            def _():
                halo_start(d, s + 1)

            @pl.when(t > 0)
            def _():
                send_out(d, s, order(t - 1))

        @pl.when(jnp.logical_and(d == 0, s < BLOCKS - 1))
        def _():
            stage_c(s + 1)

        send_out(d, s, order(NCH - 1))

    for r in (1, 2, 3):
        for c in k_copies(r, q):
            c.wait_send()
        for w in (0, 1):
            y_copy(r, w).wait_send()

    @pl.loop(0, BLOCKS)
    def _(s):
        @pl.when(q != s)
        def _():
            for w in (0, 1):
                for k in (1, 2, 3):
                    x_copy(s, k, w).wait_send()
                for k in range(4):
                    c_copy(s, k, w).wait_send()

        for d in range(DATES):
            halo_done(d, s)

            @pl.when(q != s)
            def _():
                for t in range(NCH):
                    o_copy(d, s, t).wait_send()

            @pl.when(q == s)
            def _():
                for t in range(NCH):
                    l_copy(d, s, t).wait()

        @pl.when(q != s)
        def _():
            for d in range(DATES):
                for t in range(NCH):
                    pltpu.make_async_remote_copy(
                        S.at[d, 1, pl.ds(REACH + t * CH, CH)],
                        out.at[0, DATES * s + d, pl.ds(t * CH, CH)],
                        o_send.at[d, 0, t], o_recv.at[DATES * s + d, t],
                        device_id=at(band, s), device_id_type=MESH).wait_recv()


def on_device(*args):
    any_, vmem = pl.BlockSpec(memory_space=pl.ANY), pl.BlockSpec(memory_space=pltpu.VMEM)
    dma = pltpu.SemaphoreType.DMA
    return pl.pallas_call(
        kernel,
        out_shape=jax.ShapeDtypeStruct((1, DATES * BLOCKS, R, W, C), BF),
        in_specs=[any_, vmem, vmem, vmem, vmem, vmem, any_, vmem, any_, vmem],
        out_specs=any_,
        scratch_shapes=[
            pltpu.VMEM((DATES, BLOCKS + 1, R + 2 * REACH, W, C), BF),
            pltpu.VMEM((BLOCKS, C, HID), BF),
            pltpu.VMEM((BLOCKS, HID, C), BF),
            pltpu.VMEM((BLOCKS, KS, KS, C), BF),
            pltpu.VMEM((BLOCKS, 8, HID), F32),
            pltpu.VMEM((BLOCKS, KS * KS, 8, C), BF),
            pltpu.VMEM((R * W, C), BF),
            pltpu.VMEM((CH * W, HID), BF),
            pltpu.VMEM((R * W, 128), F32),
            dma((DATES,)),
            dma((2,)),
            dma((3, 2)),
            dma((3, 2)),
            dma((BLOCKS, 2)),
            dma((BLOCKS, PIECES, 2)),
            dma((BLOCKS, 3, 2)),
            dma((BLOCKS, 4, 2)),
            dma((DATES, BLOCKS, 2)),
            dma((DATES, BLOCKS, 2)),
            dma((DATES, BLOCKS, NCH)),
            dma((DATES * BLOCKS, NCH)),
            dma((DATES, NCH)),
        ],
        compiler_params=pltpu.CompilerParams(collective_id=0, has_side_effects=True),
        name="blocks",
    )(*args)


def solution(mesh):
    in_specs = (
        P(None, "band", None, None),
        P("band", None),
        P("segment", None, None, None),
        P("segment", None),
        P("segment", None),
        P("segment", None),
        P("segment", None, None),
        P("segment", None),
        P("segment", None, None),
        P("segment", None),
    )
    return jax.shard_map(
        on_device, mesh=mesh, in_specs=in_specs,
        out_specs=P("segment", None, "band", None, None), check_vma=False,
    )
```

time: 535 us -> 105 us (0.20)
  the two profiles are of different devices: /device:TPU:29 before, /device:TPU:120 now
where the time goes in v1:
time: 105 us
  Pallas kernels  100 us (95%)
  local copies, waits for them, and re-layouts  4.79 us (5%)
    pallas_call x1, Pallas kernels, on_device(): pl.pallas_call(kernel, out_shape=jax.ShapeDtypeStruct((1, DATES * BLOCKS,...  100 us
    unnamed x1, local copies, waits for them, and re-layouts  4.79 us

profile of v1, /device:TPU:120, one launch (start us, length us, event | category | flops | bytes accessed | tf_op | source)
XLA Modules:
  0.0 104.9 jit_solution(13854498034716880682)
XLA Ops:
  0.0 100.2 %blocks.1 = bf16[1,8,16,64,256]{4,3,2,1,0:T(8,128)(2,1)} custom-call(bf16[8,16,64,256]{3,2,1,0:T(8,128)(2,1)} %fields.1, s32[16,64]{1,0:T(8,128)} %land.1, bf16[1,7,7,256]{3,2,1,0:T(8,128)(2,1)} %ck.1, bf16[1,256]{1,0:T(2,128)(2,1)} %cb.1, bf16[1,256]{1,0:T(2,128)(2,1)} %ng.1, bf16[1,256]{1,0:T(2,128)(2,1)} %ns.1, bf16[1,256,1024]{2,1,0:T(8,128)(2,1)} %up.1, ...), custom_call_target="tpu_custom_call" | custom-call | tf_op jit(solution)/shard_map/blocks/pallas_call | solution.py:385
  100.2 4.8 %copy.12 = bf16[1,8,16,64,256]{4,3,2,1,0:T(8,128)(2,1)} copy(bf16[1,8,16,64,256]{4,3,2,1,0:T(8,128)(2,1)} %blocks.1) | data formatting | bytes 8388608

commit v2 on v1

--- a/solution.py
+++ b/solution.py
@@ -20,20 +20,33 @@
     return ((p[0] + p[1]) + (p[2] + p[3])) + ((p[4] + p[5]) + p[6])
 
 
-def conv_row(state, taps, sp, normed, i):
-    xs = [state[i + a].reshape(W // 8, 8, C) for a in range(KS)]
-    acc = None
-    for b in range(KS):
-        t = tree([xs[a] * taps[a * KS + b][None] for a in range(KS)])
-        t = t.astype(F32).reshape(W, C)
-        if b != REACH:
-            t = pltpu.roll(t, (REACH - b) % W, 0)
-        acc = t if acc is None else acc + t
-    summed = acc + sp[0:1, 0:C]
-    mean = jnp.sum(summed, -1, keepdims=True) * (1.0 / C)
-    dev = summed - mean
-    var = jnp.sum(dev * dev, -1, keepdims=True) * (1.0 / C)
-    out = dev * lax.rsqrt(var + 1e-6) * sp[1:2, 0:C] + sp[2:3, 0:C]
+def conv_row(state, taps, sp, normed, i, part):
+    half = W // 2
+    for h in range(2):
+        xs = [state[i + a, h * half:(h + 1) * half].reshape(half // 8, 8, C) for a in range(KS)]
+        for b in range(KS):
+            t = tree([xs[a] * taps[a * KS + b][None] for a in range(KS)])
+            t = t.astype(F32).reshape(half, C)
+            for l in range(2):
+                tl = t[:, l * 128:(l + 1) * 128]
+                part[b, l, 8 + h * half:8 + (h + 1) * half, :] = tl
+                if h == 0 and b > REACH:
+                    part[b, l, 8 + W:16 + W, :] = tl[0:8]
+                if h == 1 and b < REACH:
+                    part[b, l, 0:8, :] = tl[half - 8:half]
+    sums = []
+    for l in range(2):
+        acc = sp[0:1, l * 128:(l + 1) * 128]
+        for b in range(KS):
+            acc = acc + part[b, l, 8 + b - REACH:8 + b - REACH + W, :]
+        sums.append(acc)
+    mean = jnp.sum(sums[0] + sums[1], -1, keepdims=True) * (1.0 / C)
+    dev = [x - mean for x in sums]
+    var = jnp.sum(dev[0] * dev[0] + dev[1] * dev[1], -1, keepdims=True) * (1.0 / C)
+    scale = lax.rsqrt(var + 1e-6)
+    out = jnp.concatenate(
+        [dev[l] * scale * sp[1:2, l * 128:(l + 1) * 128] + sp[2:3, l * 128:(l + 1) * 128]
+         for l in range(2)], axis=1)
     normed[pl.ds(pl.multiple_of(i * W, W), W), :] = out.astype(BF)
 
 
@@ -55,7 +68,7 @@
 
 
 def kernel(fields, land, ck, cb, ng, ns, up, ub, dn, db, out,
-           S, WU, WD, CK, SP, TP, N, H, MK,
+           S, WU, WD, CK, SP, TP, N, H, MK, PT,
            f_sem, own_sem, y_send, k_send, k_recv, w_recv, x_send, c_send,
            h_send, h_recv, o_send, o_recv, l_sem):
     band, q = lax.axis_index("band"), lax.axis_index("segment")
@@ -276,54 +289,36 @@
     def order(t):
         return jnp.where(t == 1, NCH - 1, jnp.where(t > 1, t - 1, 0))
 
-    @pl.loop(0, DATES * BLOCKS)
-    def _(unit):
-        d, s = unit // BLOCKS, lax.rem(unit, BLOCKS)
-        state, result = S.at[d, s], S.at[d, s + 1]
-        taps, sp, wu, wd = TP.at[s], SP.at[s], WU.at[s], WD.at[s]
-
-        @pl.when(d == 0)
-        def _():
-            @pl.when(q != s)
-            def _():
-                for w in (0, 1):
-                    pltpu.make_async_remote_copy(
-                        (CK, SP)[w].at[s], (CK, SP)[w].at[s], k_send.at[0, w], k_recv.at[s, w],
-                        device_id=at(band, seg(1)), device_id_type=MESH).wait_recv()
-
-            @pl.loop(0, KS)
-            def _(a):
-                line = CK[s, a].astype(F32)
-                for b in range(KS):
-                    taps[a * KS + b] = jnp.broadcast_to(line[b:b + 1], (8, C)).astype(BF)
-
+    def taps_of(s):
+        @pl.when(q != s)
+        def _():
+            for w in (0, 1):
+                pltpu.make_async_remote_copy(
+                    (CK, SP)[w].at[s], (CK, SP)[w].at[s], k_send.at[0, w], k_recv.at[s, w],
+                    device_id=at(band, seg(1)), device_id_type=MESH).wait_recv()
+
+        @pl.loop(0, KS)
+        def _(a):
+            line = CK[s, a].astype(F32)
+            for b in range(KS):
+                TP[s, a * KS + b] = jnp.broadcast_to(line[b:b + 1], (8, C)).astype(BF)
+
+    def conv_inner(d, s):
         @pl.loop(0, 5)
         def _(t):
-            conv_row(state, taps, sp, N, 2 * t + 3)
-            conv_row(state, taps, sp, N, 2 * t + 4)
-
-        halo_wait(d, s)
-
+            for k in range(2):
+                conv_row(S.at[d, s], TP.at[s], SP.at[s], N.at[d], 2 * t + 3 + k, PT.at[k])
+
+    def conv_outer(d, s):
         @pl.loop(0, 3)
         def _(t):
-            conv_row(state, taps, sp, N, t)
-            conv_row(state, taps, sp, N, t + 13)
-
-        @pl.when(d == 0)
-        def _():
-            @pl.when(s == 0)
-            def _():
-                stage_x(0)
-                stage_c(0)
-            stage_f(s)
-
-            @pl.when(s < BLOCKS - 1)
-            def _():
-                stage_x(s + 1)
-
+            for k in range(2):
+                conv_row(S.at[d, s], TP.at[s], SP.at[s], N.at[d], t + 13 * k, PT.at[k])
+
+    def mlp(d, s):
         @pl.loop(0, NCH)
         def _(t):
-            mlp_chunk(N, state, result, MK, wu, wd, sp, H, order(t))
+            mlp_chunk(N.at[d], S.at[d, s], S.at[d, s + 1], MK, WU.at[s], WD.at[s], SP.at[s], H, order(t))
 
             @pl.when(jnp.logical_and(t == 1, s < BLOCKS - 1))
             def _():
@@ -333,11 +328,56 @@
             def _():
                 send_out(d, s, order(t - 1))
 
-        @pl.when(jnp.logical_and(d == 0, s < BLOCKS - 1))
-        def _():
-            stage_c(s + 1)
+            @pl.when(jnp.logical_and(t == 1, jnp.logical_and(d == 0, s < BLOCKS - 2)))
+            def _():
+                stage_x(s + 2)
 
         send_out(d, s, order(NCH - 1))
+
+    taps_of(0)
+
+    @pl.loop(0, DATES)
+    def _(d):
+        conv_inner(d, 0)
+        halo_wait(d, 0)
+        conv_outer(d, 0)
+
+        @pl.when(d == 0)
+        def _():
+            stage_x(0)
+
+    stage_x(1)
+    stage_c(0)
+    stage_f(0)
+
+    @pl.loop(0, DATES)
+    def _(d):
+        mlp(d, 0)
+
+    @pl.loop(2, DATES * BLOCKS)
+    def _(unit):
+        late = unit > BLOCKS
+        d = jnp.where(late, 1, 0)
+        s = jnp.where(late, unit - BLOCKS, unit - 1)
+
+        @pl.when(d == 0)
+        def _():
+            taps_of(s)
+
+        conv_inner(d, s)
+
+        @pl.when(d == 0)
+        def _():
+            stage_c(s)
+
+        halo_wait(d, s)
+        conv_outer(d, s)
+
+        @pl.when(d == 0)
+        def _():
+            stage_f(s)
+
+        mlp(d, s)
 
     for r in (1, 2, 3):
         for c in k_copies(r, q):
@@ -380,12 +420,14 @@
 
 
 def on_device(*args):
-    any_, vmem = pl.BlockSpec(memory_space=pl.ANY), pl.BlockSpec(memory_space=pltpu.VMEM)
+    args = [pltpu.with_memory_space_constraint(a, pltpu.HBM) if i in (0, 6, 8) else a
+            for i, a in enumerate(args)]
+    any_, vmem, hbm = pl.BlockSpec(memory_space=pl.ANY), pl.BlockSpec(memory_space=pltpu.VMEM), pl.BlockSpec(memory_space=pltpu.HBM)
     dma = pltpu.SemaphoreType.DMA
     return pl.pallas_call(
         kernel,
         out_shape=jax.ShapeDtypeStruct((1, DATES * BLOCKS, R, W, C), BF),
-        in_specs=[any_, vmem, vmem, vmem, vmem, vmem, any_, vmem, any_, vmem],
+        in_specs=[hbm, vmem, vmem, vmem, vmem, vmem, hbm, vmem, hbm, vmem],
         out_specs=any_,
         scratch_shapes=[
             pltpu.VMEM((DATES, BLOCKS + 1, R + 2 * REACH, W, C), BF),
@@ -394,9 +436,10 @@
             pltpu.VMEM((BLOCKS, KS, KS, C), BF),
             pltpu.VMEM((BLOCKS, 8, HID), F32),
             pltpu.VMEM((BLOCKS, KS * KS, 8, C), BF),
-            pltpu.VMEM((R * W, C), BF),
+            pltpu.VMEM((DATES, R * W, C), BF),
             pltpu.VMEM((CH * W, HID), BF),
             pltpu.VMEM((R * W, 128), F32),
+            pltpu.VMEM((2, KS, 2, W + 16, 128), F32),
             dma((DATES,)),
             dma((2,)),
             dma((3, 2)),
@@ -411,7 +454,8 @@
             dma((DATES * BLOCKS, NCH)),
             dma((DATES, NCH)),
         ],
-        compiler_params=pltpu.CompilerParams(collective_id=0, has_side_effects=True),
+        compiler_params=pltpu.CompilerParams(
+            collective_id=0, has_side_effects=True, vmem_limit_bytes=24 << 20),
         name="blocks",
     )(*args)
 

time: 105 us -> 99.3 us (0.946)
  the two profiles are of different devices: /device:TPU:120 before, /device:TPU:24 now
where the time goes in v2:
time: 99.3 us; the launch traced here: 99 us
  Pallas kernels  92.1 us (93%)
  local copies, waits for them, and re-layouts  6.86 us (7%)
    pallas_call x1, Pallas kernels, on_device(): pl.pallas_call(kernel, out_shape=jax.ShapeDtypeStruct((1, DATES * BLOCKS,...  92.1 us
    unnamed x15, local copies, waits for them, and re-layouts  6.86 us

profile of v2, /device:TPU:24, one launch (start us, length us, event | category | flops | bytes accessed | tf_op | source)
XLA Modules:
  0.0 99.0 jit_solution(3087436720693922933)
XLA Ops:
  0.0 0.0 copy-start
  0.0 0.7 copy-done
  0.7 0.0 copy-start.1
  0.8 0.7 copy-done.1
  1.4 0.0 copy-start.2
  1.4 0.7 copy-done.2
  2.1 0.0 copy-start.3
  2.1 0.7 copy-done.3
  2.8 0.0 copy-start.4
  2.8 0.7 copy-done.4
  3.5 0.0 copy-start.5
  3.5 0.7 copy-done.5
  4.2 0.0 copy-start.6
  4.2 0.7 copy-done.6
  4.9 92.1 %blocks.1 = bf16[1,8,16,64,256]{4,3,2,1,0:T(8,128)(2,1)S(1)} custom-call(bf16[8,16,64,256]{3,2,1,0:T(8,128)(2,1)} %fields.1, s32[16,64]{1,0:T(8,128)S(1)} %copy-done.1, bf16[1,7,7,256]{3,2,1,0:T(8,128)(2,1)S(1)} %copy-done, bf16[1,256]{1,0:T(2,128)(2,1)S(1)} %copy-done.3, bf16[1,256]{1,0:T(2,128)(2,1)S(1)} %copy-done.4, bf16[1,256]{1,0:T(2,128)(2,1)S(1)} %copy-done.5, ...), custom_call_target="tpu_custom_call" | custom-call | tf_op jit(solution)/shard_map/blocks/pallas_call | solution.py:427
  97.0 2.0 %copy.12 = bf16[1,8,16,64,256]{4,3,2,1,0:T(8,128)(2,1)} copy(bf16[1,8,16,64,256]{4,3,2,1,0:T(8,128)(2,1)S(1)} %blocks.1) | data formatting | bytes 8388608
Async XLA Ops:
  0.0 0.7 copy-start
  0.7 0.7 copy-start.1
  1.4 0.7 copy-start.2
  2.1 0.7 copy-start.3
  2.8 0.7 copy-start.4
  3.5 0.7 copy-start.5
  4.2 0.7 copy-start.6

commit v3 on v2

--- a/solution.py
+++ b/solution.py
@@ -20,57 +20,53 @@
     return ((p[0] + p[1]) + (p[2] + p[3])) + ((p[4] + p[5]) + p[6])
 
 
-def conv_row(state, taps, sp, normed, i, part):
+def conv_row(state, taps, sp, shift, normed, i):
     half = W // 2
+    parts = [[], [], [], [], [], [], []]
     for h in range(2):
         xs = [state[i + a, h * half:(h + 1) * half].reshape(half // 8, 8, C) for a in range(KS)]
         for b in range(KS):
             t = tree([xs[a] * taps[a * KS + b][None] for a in range(KS)])
-            t = t.astype(F32).reshape(half, C)
-            for l in range(2):
-                tl = t[:, l * 128:(l + 1) * 128]
-                part[b, l, 8 + h * half:8 + (h + 1) * half, :] = tl
-                if h == 0 and b > REACH:
-                    part[b, l, 8 + W:16 + W, :] = tl[0:8]
-                if h == 1 and b < REACH:
-                    part[b, l, 0:8, :] = tl[half - 8:half]
-    sums = []
-    for l in range(2):
-        acc = sp[0:1, l * 128:(l + 1) * 128]
-        for b in range(KS):
-            acc = acc + part[b, l, 8 + b - REACH:8 + b - REACH + W, :]
-        sums.append(acc)
-    mean = jnp.sum(sums[0] + sums[1], -1, keepdims=True) * (1.0 / C)
-    dev = [x - mean for x in sums]
-    var = jnp.sum(dev[0] * dev[0] + dev[1] * dev[1], -1, keepdims=True) * (1.0 / C)
-    scale = lax.rsqrt(var + 1e-6)
-    out = jnp.concatenate(
-        [dev[l] * scale * sp[1:2, l * 128:(l + 1) * 128] + sp[2:3, l * 128:(l + 1) * 128]
-         for l in range(2)], axis=1)
+            parts[b].append(t.reshape(half, C))
+    stacked = jnp.concatenate([p for two in parts for p in two], axis=0)
+    summed = jnp.dot(shift[...], stacked, preferred_element_type=F32) + sp[0:1, 0:C]
+    mean = jnp.sum(summed, -1, keepdims=True) * (1.0 / C)
+    dev = summed - mean
+    var = jnp.sum(dev * dev, -1, keepdims=True) * (1.0 / C)
+    out = dev * lax.rsqrt(var + 1e-6) * sp[1:2, 0:C] + sp[2:3, 0:C]
     normed[pl.ds(pl.multiple_of(i * W, W), W), :] = out.astype(BF)
 
 
-def mlp_chunk(normed, state, result, mask, up, dn, sp, hid, ck):
+def chunk(normed, state, result, mask, up, dn, taps, sp, shift, hid, ck, after):
     m = CH * W
+    if after is not None:
+        ahead = after * CH
+    if ck is None:
+        for j in range(CH):
+            conv_row(state, taps, sp, shift, normed, ahead + j)
+        return
     r0 = pl.multiple_of(ck * m, m)
     n = normed[pl.ds(r0, m), :]
-    for j in range(4):
+    old = state[pl.ds(ck * CH + REACH, CH)]
+    for j in range(CH):
+        if after is not None:
+            conv_row(state, taps, sp, shift, normed, ahead + j)
         js = slice(j * 256, (j + 1) * 256)
         h = jnp.dot(n, up[:, js], preferred_element_type=F32) + sp[4:5, js]
         v = h.astype(BF)
         e = lax.erf(v * jnp.asarray(0.7071067811865476, BF))
         hid[:, js] = v + v * e
     u = jnp.dot(hid[...], dn[...], preferred_element_type=F32) * 0.5 + sp[3:4, 0:C]
-    st = state[pl.ds(ck * CH + REACH, CH)].reshape(m, C).astype(F32)
     mk = mask[pl.ds(r0, m), :]
-    o = (st + u) * jnp.concatenate([mk, mk], axis=1)
+    o = (old.reshape(m, C).astype(F32) + u) * jnp.concatenate([mk, mk], axis=1)
     result[pl.ds(ck * CH + REACH, CH)] = o.astype(BF).reshape(CH, W, C)
 
 
-def kernel(fields, land, ck, cb, ng, ns, up, ub, dn, db, out,
-           S, WU, WD, CK, SP, TP, N, H, MK, PT,
+def kernel(fields, land_in, ck_in, cb_in, ng_in, ns_in, up, ub_in, dn, db_in, out,
+           S, WU, WD, CK, SP, TP, N, H, MK, SH,
+           land, ck, cb, ng, ns, ub, db,
            f_sem, own_sem, y_send, k_send, k_recv, w_recv, x_send, c_send,
-           h_send, h_recv, o_send, o_recv, l_sem):
+           h_send, h_recv, o_send, o_recv, l_sem, i_sem):
     band, q = lax.axis_index("band"), lax.axis_index("segment")
     core = lax.rem(band, 2)
     xpos = band // 16
@@ -108,6 +104,11 @@
         return pltpu.make_async_copy(
             fields.at[DATES * q + d], S.at[d, 0, pl.ds(REACH, R)], f_sem.at[d])
 
+    smalls = [pltpu.make_async_copy(a, b, i_sem.at[n]) for n, (a, b) in enumerate((
+        (ck_in, ck), (cb_in, cb), (ng_in, ng), (ns_in, ns), (db_in, db), (ub_in, ub),
+        (land_in, land)))]
+    for c in smalls:
+        c.start()
     field_copy(0).start()
     field_copy(1).start()
     own_up = pltpu.make_async_copy(up.at[0], WU.at[q], own_sem.at[0])
@@ -115,6 +116,12 @@
     own_up.start()
     own_dn.start()
 
+    row_w = lax.broadcasted_iota(jnp.int32, (W, KS * W), 0)
+    col = lax.broadcasted_iota(jnp.int32, (W, KS * W), 1)
+    hit = ((row_w + (col >> 6) + (W - REACH)) & (W - 1)) == (col & (W - 1))
+    SH[...] = jnp.where(hit, 1.0, 0.0).astype(BF)
+    for c in smalls:
+        c.wait()
     CK[q] = ck[0]
     SP[q, 0:1, 0:C] = cb[...].astype(F32)
     SP[q, 1:2, 0:C] = ng[...].astype(F32)
@@ -182,9 +189,14 @@
     for r in (1, 3, 2):
         for c in k_copies(r, q):
             c.start()
-    for w in (0, 1):
-        for r in (1, 3, 2):
-            y_copy(r, w).start()
+    def y_start():
+        for w in (0, 1):
+            for r in (1, 3, 2):
+                y_copy(r, w).start()
+
+    @pl.when(q == 0)
+    def _():
+        y_start()
 
     def stage_x(s):
         @pl.when(q != s)
@@ -224,21 +236,21 @@
             S.at[d, s, src], S.at[d, s, dst], h_send.at[d, s, side], h_recv.at[d, s, side],
             device_id=at(to, q), device_id_type=MESH)
 
-    def halo_start(d, s):
-        @pl.when(has_prev)
+    def halo_start(d, s, ck):
+        @pl.when(jnp.logical_and(ck == 0, has_prev))
         def _():
             halo(d, s, 0).start()
 
-        @pl.when(has_next)
+        @pl.when(jnp.logical_and(ck == NCH - 1, has_next))
         def _():
             halo(d, s, 1).start()
 
-    def halo_wait(d, s):
-        @pl.when(has_next)
+    def halo_wait(d, s, ck):
+        @pl.when(jnp.logical_and(ck == NCH - 1, has_next))
         def _():
             halo(d, s, 0).wait_recv()
 
-        @pl.when(has_prev)
+        @pl.when(jnp.logical_and(ck == 0, has_prev))
         def _():
             halo(d, s, 1).wait_recv()
 
@@ -260,7 +272,12 @@
             x = S[d, 0, i + REACH].astype(F32) * jnp.concatenate([m, m], axis=1)
             S[d, 0, i + REACH] = x.astype(BF)
 
-        halo_start(d, 0)
+        halo_start(d, 0, 0)
+        halo_start(d, 0, NCH - 1)
+
+    @pl.when(q != 0)
+    def _():
+        y_start()
 
     def rows(ref, ck):
         return ref.at[pl.ds(ck * CH, CH)]
@@ -286,8 +303,9 @@
         def _():
             l_copy(d, s, ck).start()
 
-    def order(t):
-        return jnp.where(t == 1, NCH - 1, jnp.where(t > 1, t - 1, 0))
+    def order(s, t):
+        odd = lax.rem(s, 2) * (NCH - 1)
+        return jnp.where(t == 0, 1, jnp.where(t == 1, odd, jnp.where(t == 2, NCH - 1 - odd, 2)))
 
     def taps_of(s):
         @pl.when(q != s)
@@ -303,46 +321,42 @@
             for b in range(KS):
                 TP[s, a * KS + b] = jnp.broadcast_to(line[b:b + 1], (8, C)).astype(BF)
 
-    def conv_inner(d, s):
-        @pl.loop(0, 5)
-        def _(t):
-            for k in range(2):
-                conv_row(S.at[d, s], TP.at[s], SP.at[s], N.at[d], 2 * t + 3 + k, PT.at[k])
-
-    def conv_outer(d, s):
-        @pl.loop(0, 3)
-        def _(t):
-            for k in range(2):
-                conv_row(S.at[d, s], TP.at[s], SP.at[s], N.at[d], t + 13 * k, PT.at[k])
-
-    def mlp(d, s):
-        @pl.loop(0, NCH)
-        def _(t):
-            mlp_chunk(N.at[d], S.at[d, s], S.at[d, s + 1], MK, WU.at[s], WD.at[s], SP.at[s], H, order(t))
-
-            @pl.when(jnp.logical_and(t == 1, s < BLOCKS - 1))
-            def _():
-                halo_start(d, s + 1)
-
-            @pl.when(t > 0)
-            def _():
-                send_out(d, s, order(t - 1))
-
-            @pl.when(jnp.logical_and(t == 1, jnp.logical_and(d == 0, s < BLOCKS - 2)))
-            def _():
-                stage_x(s + 2)
-
-        send_out(d, s, order(NCH - 1))
+    def step(d, s, ck, after):
+        chunk(N.at[d], S.at[d, s], S.at[d, s + 1], MK, WU.at[s], WD.at[s], TP.at[s], SP.at[s], SH, H,
+              ck, after)
+
+    def conv(d, s, t):
+        ck = order(s, t)
+        halo_wait(d, s, ck)
+        step(d, s, None, ck)
+
+    def finish(d, s, t):
+        ck = order(s, t)
+
+        @pl.when(s < BLOCKS - 1)
+        def _():
+            halo_start(d, s + 1, ck)
+
+        @pl.when(t > 0)
+        def _():
+            send_out(d, s, order(s, t - 1))
+
+        @pl.when(jnp.logical_and(t == 2, jnp.logical_and(d == 0, s < BLOCKS - 2)))
+        def _():
+            stage_x(s + 2)
+
+        @pl.when(t == NCH - 1)
+        def _():
+            send_out(d, s, ck)
 
     taps_of(0)
 
-    @pl.loop(0, DATES)
-    def _(d):
-        conv_inner(d, 0)
-        halo_wait(d, 0)
-        conv_outer(d, 0)
-
-        @pl.when(d == 0)
+    @pl.loop(0, DATES * NCH)
+    def _(i):
+        d, t = i // NCH, lax.rem(i, NCH)
+        conv(d, 0, t)
+
+        @pl.when(i == NCH - 1)
         def _():
             stage_x(0)
 
@@ -350,9 +364,11 @@
     stage_c(0)
     stage_f(0)
 
-    @pl.loop(0, DATES)
-    def _(d):
-        mlp(d, 0)
+    @pl.loop(0, DATES * NCH)
+    def _(i):
+        d, t = i // NCH, lax.rem(i, NCH)
+        step(d, 0, order(0, t), None)
+        finish(d, 0, t)
 
     @pl.loop(2, DATES * BLOCKS)
     def _(unit):
@@ -364,20 +380,22 @@
         def _():
             taps_of(s)
 
-        conv_inner(d, s)
+        conv(d, s, 0)
 
         @pl.when(d == 0)
         def _():
             stage_c(s)
-
-        halo_wait(d, s)
-        conv_outer(d, s)
-
-        @pl.when(d == 0)
-        def _():
             stage_f(s)
 
-        mlp(d, s)
+        @pl.loop(0, NCH - 1)
+        def _(t):
+            ck, after = order(s, t), order(s, t + 1)
+            halo_wait(d, s, after)
+            step(d, s, ck, after)
+            finish(d, s, t)
+
+        step(d, s, order(s, NCH - 1), None)
+        finish(d, s, NCH - 1)
 
     for r in (1, 2, 3):
         for c in k_copies(r, q):
@@ -420,14 +438,13 @@
 
 
 def on_device(*args):
-    args = [pltpu.with_memory_space_constraint(a, pltpu.HBM) if i in (0, 6, 8) else a
-            for i, a in enumerate(args)]
-    any_, vmem, hbm = pl.BlockSpec(memory_space=pl.ANY), pl.BlockSpec(memory_space=pltpu.VMEM), pl.BlockSpec(memory_space=pltpu.HBM)
+    args = [pltpu.with_memory_space_constraint(a, pltpu.HBM) for a in args]
+    any_, hbm = pl.BlockSpec(memory_space=pl.ANY), pl.BlockSpec(memory_space=pltpu.HBM)
     dma = pltpu.SemaphoreType.DMA
     return pl.pallas_call(
         kernel,
         out_shape=jax.ShapeDtypeStruct((1, DATES * BLOCKS, R, W, C), BF),
-        in_specs=[hbm, vmem, vmem, vmem, vmem, vmem, hbm, vmem, hbm, vmem],
+        in_specs=[hbm] * 10,
         out_specs=any_,
         scratch_shapes=[
             pltpu.VMEM((DATES, BLOCKS + 1, R + 2 * REACH, W, C), BF),
@@ -439,7 +456,14 @@
             pltpu.VMEM((DATES, R * W, C), BF),
             pltpu.VMEM((CH * W, HID), BF),
             pltpu.VMEM((R * W, 128), F32),
-            pltpu.VMEM((2, KS, 2, W + 16, 128), F32),
+            pltpu.VMEM((W, KS * W), BF),
+            pltpu.VMEM((R, W), jnp.int32),
+            pltpu.VMEM((1, KS, KS, C), BF),
+            pltpu.VMEM((1, C), BF),
+            pltpu.VMEM((1, C), BF),
+            pltpu.VMEM((1, C), BF),
+            pltpu.VMEM((1, HID), BF),
+            pltpu.VMEM((1, C), BF),
             dma((DATES,)),
             dma((2,)),
             dma((3, 2)),
@@ -453,6 +477,7 @@
             dma((DATES, BLOCKS, NCH)),
             dma((DATES * BLOCKS, NCH)),
             dma((DATES, NCH)),
+            dma((7,)),
         ],
         compiler_params=pltpu.CompilerParams(
             collective_id=0, has_side_effects=True, vmem_limit_bytes=24 << 20),

time: 99.3 us -> 93.8 us (0.945)
  the two profiles are of different devices: /device:TPU:24 before, /device:TPU:29 now
where the time goes in v3:
time: 93.8 us; the launch traced here: 93.7 us
  Pallas kernels  91.7 us (98%)
  local copies, waits for them, and re-layouts  2.02 us (2%)
    pallas_call x1, Pallas kernels, on_device(): pl.pallas_call(kernel, out_shape=jax.ShapeDtypeStruct((1, DATES * BLOCKS,...  91.7 us
    unnamed x1, local copies, waits for them, and re-layouts  2.02 us

profile of v3, /device:TPU:29, one launch (start us, length us, event | category | flops | bytes accessed | tf_op | source)
XLA Modules:
  0.0 93.7 jit_solution(16825033762998016897)
XLA Ops:
  0.0 91.7 %blocks.1 = bf16[1,8,16,64,256]{4,3,2,1,0:T(8,128)(2,1)S(1)} custom-call(bf16[8,16,64,256]{3,2,1,0:T(8,128)(2,1)} %fields.1, s32[16,64]{1,0:T(8,128)} %land_in.1, bf16[1,7,7,256]{3,2,1,0:T(8,128)(2,1)} %ck_in.1, bf16[1,256]{1,0:T(2,128)(2,1)} %cb_in.1, bf16[1,256]{1,0:T(2,128)(2,1)} %ng_in.1, bf16[1,256]{1,0:T(2,128)(2,1)} %ns_in.1, ...), custom_call_target="tpu_custom_call" | custom-call | tf_op jit(solution)/shard_map/blocks/pallas_call | solution.py:444
  91.7 2.0 %copy.12 = bf16[1,8,16,64,256]{4,3,2,1,0:T(8,128)(2,1)} copy(bf16[1,8,16,64,256]{4,3,2,1,0:T(8,128)(2,1)S(1)} %blocks.1) | data formatting | bytes 8388608

commit v4 on v3

--- a/solution.py
+++ b/solution.py
@@ -66,7 +66,7 @@
            S, WU, WD, CK, SP, TP, N, H, MK, SH,
            land, ck, cb, ng, ns, ub, db,
            f_sem, own_sem, y_send, k_send, k_recv, w_recv, x_send, c_send,
-           h_send, h_recv, o_send, o_recv, l_sem, i_sem):
+           h_send, h_recv, o_send, o_recv, l_sem, i_sem, RL, rl_send, rl_recv):
     band, q = lax.axis_index("band"), lax.axis_index("segment")
     core = lax.rem(band, 2)
     xpos = band // 16
@@ -294,8 +294,33 @@
             S.at[d, s + 1, pl.ds(REACH + ck * CH, CH)],
             out.at[0, DATES * q + d, pl.ds(ck * CH, CH)], l_sem.at[d, ck])
 
+    relayed = jnp.logical_and(q == 1, core == 1)
+    relays = jnp.logical_and(q == 2, core == 1)
+
+    def relay_in(d, ck):
+        return pltpu.make_async_remote_copy(
+            S.at[d, BLOCKS, pl.ds(REACH + ck * CH, CH)], RL.at[d, pl.ds(ck * CH, CH)],
+            o_send.at[d, BLOCKS - 1, ck], rl_recv.at[d, ck],
+            device_id=at(band, 2), device_id_type=MESH)
+
+    def relay_out(d, ck):
+        return pltpu.make_async_remote_copy(
+            RL.at[d, pl.ds(ck * CH, CH)], out.at[0, DATES + d, pl.ds(ck * CH, CH)],
+            rl_send.at[d, ck], o_recv.at[DATES + d, ck],
+            device_id=at(band, BLOCKS - 1), device_id_type=MESH)
+
+    def relay(d, ck):
+        relay_in(d, ck).wait_recv()
+        relay_out(d, ck).start()
+
     def send_out(d, s, ck):
-        @pl.when(q != s)
+        by_relay = jnp.logical_and(relayed, s == BLOCKS - 1)
+
+        @pl.when(by_relay)
+        def _():
+            relay_in(d, ck).start()
+
+        @pl.when(jnp.logical_and(q != s, jnp.logical_not(by_relay)))
         def _():
             o_copy(d, s, ck).start()
 
@@ -341,9 +366,9 @@
         def _():
             send_out(d, s, order(s, t - 1))
 
-        @pl.when(jnp.logical_and(t == 2, jnp.logical_and(d == 0, s < BLOCKS - 2)))
-        def _():
-            stage_x(s + 2)
+        @pl.when(jnp.logical_and(relays, jnp.logical_and(d == 1, s == 2)))
+        def _():
+            relay(0, order(BLOCKS - 1, t))
 
         @pl.when(t == NCH - 1)
         def _():
@@ -363,6 +388,7 @@
     stage_x(1)
     stage_c(0)
     stage_f(0)
+    stage_x(2)
 
     @pl.loop(0, DATES * NCH)
     def _(i):
@@ -370,6 +396,12 @@
         step(d, 0, order(0, t), None)
         finish(d, 0, t)
 
+        @pl.when(i == NCH + 1)
+        def _():
+            stage_c(1)
+
+    stage_x(3)
+
     @pl.loop(2, DATES * BLOCKS)
     def _(unit):
         late = unit > BLOCKS
@@ -384,7 +416,6 @@
 
         @pl.when(d == 0)
         def _():
-            stage_c(s)
             stage_f(s)
 
         @pl.loop(0, NCH - 1)
@@ -397,11 +428,26 @@
         step(d, s, order(s, NCH - 1), None)
         finish(d, s, NCH - 1)
 
+        @pl.when(jnp.logical_and(d == 0, s < BLOCKS - 1))
+        def _():
+            stage_c(s + 1)
+
+    @pl.when(relays)
+    def _():
+        for t in range(NCH):
+            relay(1, order(BLOCKS - 1, t))
+
     for r in (1, 2, 3):
         for c in k_copies(r, q):
             c.wait_send()
         for w in (0, 1):
             y_copy(r, w).wait_send()
+
+    @pl.when(relays)
+    def _():
+        for d in range(DATES):
+            for t in range(NCH):
+                relay_out(d, t).wait_send()
 
     @pl.loop(0, BLOCKS)
     def _(s):
@@ -478,6 +524,9 @@
             dma((DATES * BLOCKS, NCH)),
             dma((DATES, NCH)),
             dma((7,)),
+            pltpu.VMEM((DATES, R, W, C), BF),
+            dma((DATES, NCH)),
+            dma((DATES, NCH)),
         ],
         compiler_params=pltpu.CompilerParams(
             collective_id=0, has_side_effects=True, vmem_limit_bytes=24 << 20),

time: 93.8 us -> 106 us (1.13)
  Pallas kernels: 91.7 us -> 104 us
    pallas_call x1, Pallas kernels: 91.7 us -> 104 us  [on_device(): pl.pallas_call(kernel, out_shape=jax.ShapeDtypeStruct((1, DATES * BLOCKS,...]
where the time goes in v4:
time: 106 us
  Pallas kernels  104 us (98%)
  local copies, waits for them, and re-layouts  2.02 us (2%)
    pallas_call x1, Pallas kernels, on_device(): pl.pallas_call(kernel, out_shape=jax.ShapeDtypeStruct((1, DATES * BLOCKS,...  104 us

profile of v4, /device:TPU:29, one launch (start us, length us, event | category | flops | bytes accessed | tf_op | source)
XLA Modules:
  0.0 106.3 jit_solution(5222014419881243000)
XLA Ops:
  0.0 104.3 %blocks.1 = bf16[1,8,16,64,256]{4,3,2,1,0:T(8,128)(2,1)S(1)} custom-call(bf16[8,16,64,256]{3,2,1,0:T(8,128)(2,1)} %fields.1, s32[16,64]{1,0:T(8,128)} %land_in.1, bf16[1,7,7,256]{3,2,1,0:T(8,128)(2,1)} %ck_in.1, bf16[1,256]{1,0:T(2,128)(2,1)} %cb_in.1, bf16[1,256]{1,0:T(2,128)(2,1)} %ng_in.1, bf16[1,256]{1,0:T(2,128)(2,1)} %ns_in.1, ...), custom_call_target="tpu_custom_call" | custom-call | tf_op jit(solution)/shard_map/blocks/pallas_call | solution.py:490
  104.3 2.0 %copy.12 = bf16[1,8,16,64,256]{4,3,2,1,0:T(8,128)(2,1)} copy(bf16[1,8,16,64,256]{4,3,2,1,0:T(8,128)(2,1)S(1)} %blocks.1) | data formatting | bytes 8388608

commit v5 on v3

--- a/solution.py
+++ b/solution.py
@@ -116,10 +116,49 @@
     own_up.start()
     own_dn.start()
 
-    row_w = lax.broadcasted_iota(jnp.int32, (W, KS * W), 0)
-    col = lax.broadcasted_iota(jnp.int32, (W, KS * W), 1)
-    hit = ((row_w + (col >> 6) + (W - REACH)) & (W - 1)) == (col & (W - 1))
-    SH[...] = jnp.where(hit, 1.0, 0.0).astype(BF)
+    def k_copies(r, s):
+        return (
+            pltpu.make_async_remote_copy(
+                CK.at[s], CK.at[s], k_send.at[r - 1, 0], k_recv.at[s, 0],
+                device_id=at(band, seg(r)), device_id_type=MESH),
+            pltpu.make_async_remote_copy(
+                SP.at[s], SP.at[s], k_send.at[r - 1, 1], k_recv.at[s, 1],
+                device_id=at(band, seg(r)), device_id_type=MESH))
+
+    def part(ref, s, p, w):
+        n = (UPR, DNR)[w]
+        return ref.at[s, pl.ds(pl.multiple_of(p * n, n), n)]
+
+    def y_copy(r, w):
+        return pltpu.make_async_remote_copy(
+            part((up, dn)[w], 0, mine, w), part((WU, WD)[w], q, mine, w),
+            y_send.at[r - 1, w], w_recv.at[q, mine, w],
+            device_id=at(band, seg(r)), device_id_type=MESH)
+
+    def w_copy(s, p, w, b, sem):
+        ref = (WU, WD)[w]
+        return pltpu.make_async_remote_copy(
+            part(ref, s, p, w), part(ref, s, p, w), sem, w_recv.at[s, p, w],
+            device_id=at(b, q), device_id_type=MESH)
+
+    def x_copy(s, k, w):
+        return w_copy(s, mine, w, x_band(k), x_send.at[s, k - 1, w])
+
+    def c_copy(s, k, w):
+        p = 2 * lax.rem(xpos + k, 4) + core
+        return w_copy(s, p, w, sib, c_send.at[s, k, w])
+
+    pl.semaphore_wait(barrier, 7 + has_other.astype(jnp.int32))
+
+    def y_start():
+        for w in (0, 1):
+            for r in (1, 3, 2):
+                y_copy(r, w).start()
+
+    @pl.when(q == 0)
+    def _():
+        y_start()
+
     for c in smalls:
         c.wait()
     CK[q] = ck[0]
@@ -129,14 +168,21 @@
     SP[q, 3:4, 0:C] = db[...].astype(F32)
     SP[q, 4:5, :] = ub[...].astype(F32)
 
+    row_w = lax.broadcasted_iota(jnp.int32, (W, KS * W), 0)
+    col = lax.broadcasted_iota(jnp.int32, (W, KS * W), 1)
+    hit = ((row_w + (col >> 6) + (W - REACH)) & (W - 1)) == (col & (W - 1))
+    SH[...] = jnp.where(hit, 1.0, 0.0).astype(BF)
+    for r in (1, 3, 2):
+        for c in k_copies(r, q):
+            c.start()
+
     eye = (lax.broadcasted_iota(jnp.int32, (W, W), 0)
            == lax.broadcasted_iota(jnp.int32, (W, W), 1))
 
-    @pl.loop(0, R)
-    def _(i):
-        row = jnp.broadcast_to(land[pl.ds(i, 1), :].astype(F32), (W, W))
-        col = jnp.sum(jnp.where(eye, row, 0.0), -1, keepdims=True)
-        MK[pl.ds(pl.multiple_of(i * W, W), W), :] = jnp.broadcast_to(col, (W, 128))
+    for i in range(R):
+        row = jnp.broadcast_to(land[i:i + 1, :].astype(F32), (W, W))
+        line = jnp.sum(jnp.where(eye, row, 0.0), -1, keepdims=True)
+        MK[i * W:(i + 1) * W, :] = jnp.broadcast_to(line, (W, 128))
 
     edge = jnp.zeros((REACH, W, C), BF)
 
@@ -152,56 +198,10 @@
         def _(t):
             S[t // BLOCKS, lax.rem(t, BLOCKS), R + REACH:R + 2 * REACH] = edge
 
-    pl.semaphore_wait(barrier, 7 + has_other.astype(jnp.int32))
-
-    def k_copies(r, s):
-        return (
-            pltpu.make_async_remote_copy(
-                CK.at[s], CK.at[s], k_send.at[r - 1, 0], k_recv.at[s, 0],
-                device_id=at(band, seg(r)), device_id_type=MESH),
-            pltpu.make_async_remote_copy(
-                SP.at[s], SP.at[s], k_send.at[r - 1, 1], k_recv.at[s, 1],
-                device_id=at(band, seg(r)), device_id_type=MESH))
-
-    def part(ref, s, p, w):
-        n = (UPR, DNR)[w]
-        return ref.at[s, pl.ds(pl.multiple_of(p * n, n), n)]
-
-    def y_copy(r, w):
-        return pltpu.make_async_remote_copy(
-            part((up, dn)[w], 0, mine, w), part((WU, WD)[w], q, mine, w),
-            y_send.at[r - 1, w], w_recv.at[q, mine, w],
-            device_id=at(band, seg(r)), device_id_type=MESH)
-
-    def w_copy(s, p, w, b, sem):
-        ref = (WU, WD)[w]
-        return pltpu.make_async_remote_copy(
-            part(ref, s, p, w), part(ref, s, p, w), sem, w_recv.at[s, p, w],
-            device_id=at(b, q), device_id_type=MESH)
-
-    def x_copy(s, k, w):
-        return w_copy(s, mine, w, x_band(k), x_send.at[s, k - 1, w])
-
-    def c_copy(s, k, w):
-        p = 2 * lax.rem(xpos + k, 4) + core
-        return w_copy(s, p, w, sib, c_send.at[s, k, w])
-
-    for r in (1, 3, 2):
-        for c in k_copies(r, q):
-            c.start()
-    def y_start():
-        for w in (0, 1):
-            for r in (1, 3, 2):
-                y_copy(r, w).start()
-
-    @pl.when(q == 0)
-    def _():
-        y_start()
-
-    def stage_x(s):
-        @pl.when(q != s)
-        def _():
-            for w in (0, 1):
+    def stage_x(s, halves=(0, 1)):
+        @pl.when(q != s)
+        def _():
+            for w in halves:
                 c_copy(s, 0, w).wait_recv()
                 for k in (1, 3, 2):
                     x_copy(s, k, w).start()
@@ -341,9 +341,13 @@
         def _():
             send_out(d, s, order(s, t - 1))
 
-        @pl.when(jnp.logical_and(t == 2, jnp.logical_and(d == 0, s < BLOCKS - 2)))
-        def _():
-            stage_x(s + 2)
+        @pl.when(jnp.logical_and(t == 2, jnp.logical_and(d == 0, s == 0)))
+        def _():
+            @pl.when(q == 3)
+            def _():
+                stage_x(2)
+
+            stage_x(3)
 
         @pl.when(t == NCH - 1)
         def _():
@@ -356,19 +360,33 @@
         d, t = i // NCH, lax.rem(i, NCH)
         conv(d, 0, t)
 
-        @pl.when(i == NCH - 1)
-        def _():
-            stage_x(0)
-
-    stage_x(1)
+        @pl.when(i == 0)
+        def _():
+            stage_x(0, (0,))
+
+        @pl.when(i == 2)
+        def _():
+            stage_x(0, (1,))
+
+        @pl.when(i == 5)
+        def _():
+            stage_x(1)
+
+    @pl.when(q < 2)
+    def _():
+        stage_x(2)
+
     stage_c(0)
     stage_f(0)
 
-    @pl.loop(0, DATES * NCH)
-    def _(i):
-        d, t = i // NCH, lax.rem(i, NCH)
-        step(d, 0, order(0, t), None)
-        finish(d, 0, t)
+    def matmuls(d, s):
+        @pl.loop(0, NCH)
+        def _(t):
+            step(d, s, order(s, t), None)
+            finish(d, s, t)
+
+    matmuls(0, 0)
+    stage_c(1)
 
     @pl.loop(2, DATES * BLOCKS)
     def _(unit):
@@ -380,11 +398,14 @@
         def _():
             taps_of(s)
 
+        @pl.when(unit == BLOCKS + 1)
+        def _():
+            matmuls(1, 0)
+
         conv(d, s, 0)
 
         @pl.when(d == 0)
         def _():
-            stage_c(s)
             stage_f(s)
 
         @pl.loop(0, NCH - 1)
@@ -396,6 +417,10 @@
 
         step(d, s, order(s, NCH - 1), None)
         finish(d, s, NCH - 1)
+
+        @pl.when(jnp.logical_and(d == 0, s < BLOCKS - 1))
+        def _():
+            stage_c(s + 1)
 
     for r in (1, 2, 3):
         for c in k_copies(r, q):

time: 93.8 us -> 90.8 us (0.968)
  the two profiles are of different devices: /device:TPU:29 before, /device:TPU:1 now
where the time goes in v5:
time: 90.8 us; the launch traced here: 90.7 us
  Pallas kernels  88.7 us (98%)
  local copies, waits for them, and re-layouts  2.02 us (2%)
    pallas_call x1, Pallas kernels, on_device(): pl.pallas_call(kernel, out_shape=jax.ShapeDtypeStruct((1, DATES * BLOCKS,...  88.7 us
    unnamed x1, local copies, waits for them, and re-layouts  2.02 us

profile of v5, /device:TPU:1, one launch (start us, length us, event | category | flops | bytes accessed | tf_op | source)
XLA Modules:
  0.0 90.7 jit_solution(6103144307954615627)
XLA Ops:
  0.0 88.7 %blocks.1 = bf16[1,8,16,64,256]{4,3,2,1,0:T(8,128)(2,1)S(1)} custom-call(bf16[8,16,64,256]{3,2,1,0:T(8,128)(2,1)} %fields.1, s32[16,64]{1,0:T(8,128)} %land_in.1, bf16[1,7,7,256]{3,2,1,0:T(8,128)(2,1)} %ck_in.1, bf16[1,256]{1,0:T(2,128)(2,1)} %cb_in.1, bf16[1,256]{1,0:T(2,128)(2,1)} %ng_in.1, bf16[1,256]{1,0:T(2,128)(2,1)} %ns_in.1, ...), custom_call_target="tpu_custom_call" | custom-call | tf_op jit(solution)/shard_map/blocks/pallas_call | solution.py:469
  88.7 2.0 %copy.12 = bf16[1,8,16,64,256]{4,3,2,1,0:T(8,128)(2,1)} copy(bf16[1,8,16,64,256]{4,3,2,1,0:T(8,128)(2,1)S(1)} %blocks.1) | data formatting | bytes 8388608
